TPU v7x, 128 devices: a whole 4x4x4 slice. The times are simulated.
128 devices in a mesh: row: 8 (over x_hi, y), col: 16 (over z, x_lo, core).
Axes of the slice: x: 4 (x_hi: 2, x_lo: 2; x = x_hi * 2 + x_lo), y: 4, z: 4, core: 2. Of those that a mesh axis runs over, the one named last changes fastest.
Arguments:
- amplitudes: bfloat16 [32, 256, 32, 256], P('row', None, 'col'), may hold values from -6 to 6
- factors: bfloat16 [32, 256, 384], P('row'), may hold values from -0.109375 to 0.109375
- occ_energy: float32 [32], replicated, may hold values from -2 to -0.5
- vir_energy: float32 [256], replicated, may hold values from 0.2 to 3
Outputs:
- residual: float32 [32, 256, 32, 256], P('row', None, 'col')
All inputs are finite; a program needn't handle non-finite values.
Results may differ from a plain program's by a relative error of at most 0.0029.
Values may be sent and summed in bfloat16 or wider, within the bound.
No kernel may reach another device: no remote copies, remote signals or barrier semaphores. Data moves between devices by JAX's collectives and lax.ppermute only.
A program may use at most 192 MiB of HBM per device.

v0:
```python
import functools

import jax
import jax.numpy as jnp
from jax import lax
from jax.experimental import pallas as pl
from jax.experimental.pallas import tpu as pltpu
from jax.sharding import PartitionSpec as P


F32, BF16 = jnp.float32, jnp.bfloat16
VMEM = pl.BlockSpec(memory_space=pltpu.VMEM)
SMEM = pl.BlockSpec(memory_space=pltpu.SMEM)
AXES = ("row", "col")

X_HI, Y, Z, X_LO, CORE = 2, 4, 4, 2, 2


def permutation(move):
    pairs = []
    for x_hi in range(X_HI):
        for y in range(Y):
            for z in range(Z):
                for x_lo in range(X_LO):
                    for core in range(CORE):
                        h, w, d, l, c = move(x_hi, y, z, x_lo, core)
                        source = (x_hi * Y + y) * (Z * X_LO * CORE) + (z * X_LO + x_lo) * CORE + core
                        target = (h * Y + w) * (Z * X_LO * CORE) + (d * X_LO + l) * CORE + c
                        pairs.append((source, target))
    return pairs


def send(value, move):
    return lax.ppermute(value, AXES, permutation(move))


def along_y(step):
    return lambda h, y, z, l, c: (h, (y + step) % Y, z, l, c)


def other_half(h, y, z, l, c):
    return (1 - h, y, z, l, c)


def other_core(h, y, z, l, c):
    return (h, y, z, l, 1 - c)


def along_z(step):
    return lambda h, y, z, l, c: (h, y, (z + step) % Z, l, c)


def mirror_from(h, y, z, l, c):
    chip_row, chip_col = h * Y + y, z * X_LO + l
    return (chip_col // Y, chip_col % Y, chip_row // X_LO, chip_row % X_LO, c)


def turned_z(h, y, z, l):
    return z ^ ((l ^ (y % 2)) * 2 + h)


def spread(turn):
    return lambda h, y, z, l, c: (h, y, turned_z(h, y, z, l), l, c ^ turn)


def mirror_rest(h, y, z, l, c):
    return mirror_from(h, y, turned_z(h, y, z, l), l, c)


def mirror_whole(turn):
    return lambda h, y, z, l, c: mirror_from(h, y, z, l, c ^ turn)


def call(kernel, out_shape, operands, flops, specs=None, scratch=(), alias=None):
    return pl.pallas_call(
        kernel,
        out_shape=out_shape,
        in_specs=specs or [VMEM] * len(operands),
        out_specs=VMEM,
        scratch_shapes=scratch,
        input_output_aliases=alias or {},
        compiler_params=pltpu.CompilerParams(vmem_limit_bytes=6 << 20),
        cost_estimate=pl.CostEstimate(flops=flops, bytes_accessed=1 << 20, transcendentals=0),
    )(*operands)


def couple_all(left, right, out):
    left_count, virtual, aux = left.shape
    rows = left[...].reshape(left_count * virtual, aux)
    for k in range(right.shape[0]):
        both = lax.dot_general(rows, right[k], (((1,), (1,)), ((), ())), preferred_element_type=F32)
        for i in range(left_count):
            at = slice(i * virtual, (i + 1) * virtual)
            out[at, k * virtual : (k + 1) * virtual] = (2.0 * both[at] - both[at].T).astype(BF16)


def couple_whole_kernel(left, right, out):
    couple_all(left, right, out)


def fill_left(core, moved, swapped, left):
    half = moved.shape[0]
    left[pl.ds(core * half, half)] = moved[...]
    left[pl.ds((1 - core) * half, half)] = swapped[...]


def fill_right(core, z, moved, swapped, right):
    part = moved.shape[1]
    blocks = moved.shape[0] // Z
    for shift in range(Z):
        orbital = lax.rem(z - shift + Z, Z)
        for block in range(blocks):
            to = block * Z + orbital
            at = shift * blocks + block
            right[to, pl.ds(pl.multiple_of(core * part, part), part), :] = moved[at]
            right[to, pl.ds(pl.multiple_of((1 - core) * part, part), part), :] = swapped[at]


def couple_other_own_kernel(place, moved, swapped, right, out, left):
    fill_left(place[0], moved, swapped, left)
    couple_all(left, right, out)


def couple_other_rest_kernel(place, moved, swapped, right_moved, right_swapped, out, left, right):
    fill_left(place[0], moved, swapped, left)
    fill_right(place[0], place[1], right_moved, right_swapped, right)
    couple_all(left, right, out)


def couple_mine_rest_kernel(place, left, right_moved, right_swapped, out, right):
    fill_right(place[0], place[1], right_moved, right_swapped, right)
    couple_all(left, right, out)


def couple(kernel, operands, left_count, right_count, virtual, aux, scratch=()):
    shape = jax.ShapeDtypeStruct((left_count * virtual, right_count * virtual), BF16)
    flops = 2 * left_count * right_count * virtual * virtual * aux
    specs = [SMEM if o.dtype == jnp.int32 else VMEM for o in operands]
    scratch = [pltpu.VMEM((n, virtual, aux), BF16) for n in scratch]
    return call(kernel, shape, operands, flops, specs=specs, scratch=scratch)


def product_kernel(spans, has_sum, *refs):
    out = refs[-1]
    lefts, amps = refs[: len(spans)], refs[len(spans) : 2 * len(spans)]
    total = refs[-2][...] if has_sum else None
    for left, amp, (start, stop) in zip(lefts, amps, spans):
        term = jnp.dot(left[:, start:stop], amp[...], preferred_element_type=F32)
        total = term if total is None else total + term
    out[...] = total.astype(out.dtype)


def product(pieces, before=None, out_dtype=F32):
    lefts, starts, amps = zip(*pieces)
    spans = tuple((s, s + a.shape[0]) for s, a in zip(starts, amps))
    rows, width = lefts[0].shape[0], amps[0].shape[1]
    operands = [*lefts, *amps] + ([] if before is None else [before])
    alias = None if before is None or out_dtype != F32 else {len(operands) - 1: 0}
    flops = 2 * rows * width * sum(b - a for a, b in spans)
    kernel = functools.partial(product_kernel, spans, before is not None)
    return call(kernel, jax.ShapeDtypeStruct((rows, width), out_dtype), operands, flops, alias=alias)


def pack_kernel(*refs):
    parts, out = refs[:-1], refs[-1]
    size = parts[0].shape[0]
    for index, part in enumerate(parts):
        out[index * size : (index + 1) * size] = part[...]


def pack(parts):
    first = parts[0]
    shape = jax.ShapeDtypeStruct((len(parts) * first.shape[0], *first.shape[1:]), first.dtype)
    return call(pack_kernel, shape, parts, 1)


def spread_rows(value, out, index, lanes):
    virtual = value.shape[0]
    cuts = virtual // lanes
    for cut in range(cuts):
        out[pl.ds(cut * 2 + index, virtual, stride=2 * cuts), :] = value[:, cut * lanes : (cut + 1) * lanes]


def round_kernel(place, mine, received, same, other, turned):
    rows, virtual = mine.shape[0] // 2, mine.shape[1]
    for out, side in ((same, place[0]), (other, 1 - place[0])):
        for orbital in range(2):
            at = pl.ds(pl.multiple_of(side * rows + orbital * virtual, virtual), virtual)
            spread_rows((mine[at, :] + received[at, :].astype(F32)).T, turned, orbital, out.shape[1])
        out[...] = turned[...].astype(BF16)


def round_halves(place, mine, received, lanes):
    size = mine.size // 2
    half = jax.ShapeDtypeStruct((size // lanes, lanes), BF16)
    return pl.pallas_call(
        round_kernel,
        out_shape=[half, half],
        in_specs=[SMEM, VMEM, VMEM],
        out_specs=[VMEM, VMEM],
        scratch_shapes=[pltpu.VMEM(half.shape, F32)],
        compiler_params=pltpu.CompilerParams(vmem_limit_bytes=4 << 20),
        cost_estimate=pl.CostEstimate(flops=mine.size, bytes_accessed=6 * mine.size, transcendentals=0),
        name="round",
    )(place, mine, received)


def prepare_kernel(occ_first, occ_second, vir_col, vir_row, *refs):
    sums, received, base, inverse = refs[:2], refs[2:4], refs[4], refs[5]
    virtual = vir_col.shape[0]
    count = sums[0].shape[0] // virtual
    size = base.shape[0] // count
    for i in range(count):
        rows = slice(i * virtual, (i + 1) * virtual)
        for j in range(2):
            share = 1.0 / (vir_col[...] + vir_row[...] - occ_first[i] - occ_second[j])
            total = (sums[j][rows, :] + received[j][rows, :].astype(F32)) * share
            spread_rows(total, base.at[i * size : (i + 1) * size], j, base.shape[1])
            spread_rows(share, inverse.at[i * size : (i + 1) * size], j, base.shape[1])


def final_kernel(place, base, inverse, early_both, late_same, late_other, out):
    size = out.shape[0]
    early_same, early_other = early_both.at[:size], early_both.at[size:]
    step = pl.program_id(0)
    early = step < 2
    same = place[0] == lax.rem(step, 2)

    def finish(mirrored):
        out[...] = base[...] + mirrored[...].astype(F32) * inverse[...]

    for ref, first, own in (
        (early_same, True, True),
        (early_other, True, False),
        (late_same, False, True),
        (late_other, False, False),
    ):
        @pl.when((early == first) & (same == own))
        def _():
            finish(ref)


def inner(amplitudes, factors, occ_energy, vir_energy):
    own_rows, virtual, aux = factors.shape
    pairs_cols = amplitudes.shape[2]
    row, col = lax.axis_index("row"), lax.axis_index("col")
    core, z = lax.rem(col, CORE), col // (X_LO * CORE)
    place = jnp.stack([core, z])
    depth = own_rows * virtual
    half, part = own_rows // 2, virtual // CORE

    piece = lax.dynamic_slice(factors, (z, core * part, 0), (1, part, aux))
    pieces = [send(piece, along_y(s)) for s in (1, -1, 2)]
    left_moved = send(lax.dynamic_slice_in_dim(factors, core * half, half, 0), other_half)

    whole = amplitudes.reshape(depth, pairs_cols * virtual)
    own = [whole[:, j * virtual : (j + 1) * virtual] for j in range(pairs_cols)]
    prev, next_ = [], []
    for j in range(pairs_cols):
        prev.append(send(own[j], along_y(1)))
        next_.append(send(own[j], along_y(-1)))
    pieces = pack(pieces)
    eighths = [pieces] + [send(pieces, along_z(s)) for s in (1, 2, 3)]
    left_swapped = send(left_moved, other_core)
    right_moved = pack(eighths)
    right_swapped = send(right_moved, other_core)
    far = [send(prev[0], along_y(1))]
    far.append(send(next_[1], along_y(-1)))

    count, rest = own_rows, 3 * own_rows
    coupling = {}
    coupling["mine", "own"] = couple(couple_whole_kernel, [factors, factors], count, count, virtual, aux)
    coupling["other", "own"] = couple(
        couple_other_own_kernel, [place, left_moved, left_swapped, factors], count, count, virtual, aux, (count,)
    )
    operands = [place, left_moved, left_swapped, right_moved, right_swapped]
    coupling["other", "rest"] = couple(
        couple_other_rest_kernel, operands, count, rest, virtual, aux, (count, rest)
    )
    operands = [place, factors, right_moved, right_swapped]
    coupling["mine", "rest"] = couple(couple_mine_rest_kernel, operands, count, rest, virtual, aux, (rest,))

    def sums_of(name, j, dtype):
        rest = coupling[name, "rest"]
        pieces = [(rest, 0, prev[j]), (rest, depth, next_[j]), (rest, 2 * depth, far[j])]
        return product([(coupling[name, "own"], 0, own[j]), *pieces], None, dtype)

    sums, received, mirrored = [], [], []
    for j in range(pairs_cols):
        other = sums_of("other", j, BF16)
        received.append(send(other, other_half))
        sums.append(sums_of("mine", j, F32))
    lanes = 128
    cuts = virtual // lanes
    for j in range(pairs_cols):
        same, other = round_halves(place, sums[j], received[j], lanes)
        if j == 0:
            halves = [send(same, spread(0)), send(other, spread(1))]
            mirrored.append(send(pack(halves), mirror_rest))
            continue
        mirrored += [send(same, mirror_whole(0)), send(other, mirror_whole(1))]

    occ_first = lax.dynamic_slice_in_dim(occ_energy, row * own_rows, own_rows, 0)
    occ_second = lax.dynamic_slice_in_dim(occ_energy, col * pairs_cols, pairs_cols, 0)
    shape = jax.ShapeDtypeStruct((depth * cuts * pairs_cols, lanes), F32)
    operands = [vir_energy[:, None], vir_energy[None, :], *sums, *received]
    base, inverse = pl.pallas_call(
        prepare_kernel,
        out_shape=[shape, shape],
        in_specs=[SMEM] * 2 + [VMEM] * len(operands),
        out_specs=[VMEM, VMEM],
        compiler_params=pltpu.CompilerParams(vmem_limit_bytes=4 << 20),
        cost_estimate=pl.CostEstimate(flops=4 * shape.size, bytes_accessed=10 * shape.size, transcendentals=0),
        name="prepare",
    )(occ_first, occ_second, *operands)
    block = shape.shape[0] // own_rows

    def orbital_of(step, place):
        return (lax.rem(step, 2) * 2 + step // 2, 0)

    by_orbital = pl.BlockSpec((block, lanes), orbital_of)
    out = pl.pallas_call(
        final_kernel,
        out_shape=shape,
        grid_spec=pltpu.PrefetchScalarGridSpec(
            num_scalar_prefetch=1,
            grid=(own_rows,),
            in_specs=[by_orbital] * 2 + [pl.BlockSpec(m.shape, lambda step, place: (0, 0)) for m in mirrored],
            out_specs=by_orbital,
        ),
        compiler_params=pltpu.CompilerParams(vmem_limit_bytes=12 << 20),
        cost_estimate=pl.CostEstimate(flops=2 * shape.size, bytes_accessed=12 * shape.size, transcendentals=0),
        name="finish",
    )(place, base, inverse, *mirrored)
    out = out.reshape(own_rows, virtual, cuts, pairs_cols, lanes).transpose(0, 1, 3, 2, 4)
    return out.reshape(own_rows, virtual, pairs_cols, virtual)


def solution(mesh):
    in_specs = (P("row", None, "col", None), P("row", None, None), P(), P())
    out_specs = P("row", None, "col", None)
    return jax.shard_map(inner, mesh=mesh, in_specs=in_specs, out_specs=out_specs, check_vma=False)
```

profile of v0, /device:TPU:13, one launch (start us, length us, event | category | flops | bytes accessed | tf_op | source)
XLA Modules:
  0.0 144.2 jit_solution(15387648561637868955)
XLA Ops:
  0.0 1.0 constant_dynamic-slice_fusion.1
  1.0 1.4 collective-permute-start
  2.4 0.2 collective-permute-start.1
  2.6 2.0 %collective-permute-start.2 = (bf16[1,128,384]{2,1,0:T(8,128)(2,1)S(1)}, bf16[1,128,384]{2,1,0:T(8,128)(2,1)S(1)}, u32[]{:S(2)}, u32[]{:S(2)}) collective-permute-start(bf16[1,128,384]{2,1,0:T(8,128)(2,1)S(1)} %constant_dynamic-slice_fusion.1), channel_id=1, source_target_pairs={{0,32},{1,33},{2,34},{3,35},{4,36},{5,37},{6,38},{7,39},{8,40},{9,... | collective-permute-start | bytes 294920 | tf_op jit(solution)/shard_map/ppermute | solution.py:34
  4.6 0.0 collective-permute-done.refs_0_
  4.6 1.4 collective-permute-done.1.refs_1_
  6.0 2.3 %collective-permute-done.2.refs_2_ = bf16[1,128,384]{2,1,0:T(8,128)(2,1)S(1)} collective-permute-done((bf16[1,128,384]{2,1,0:T(8,128)(2,1)S(1)}, bf16[1,128,384]{2,1,0:T(8,128)(2,1)S(1)}, u32[]{:S(2)}, u32[]{:S(2)}) %collective-permute-start.2) | collective-permute-done | bytes 98336 | tf_op jit(solution)/shard_map/ppermute | solution.py:34
  8.4 1.7 %collective-permute-start.3 = (bf16[3,128,384]{2,1,0:T(8,128)(2,1)S(1)}, bf16[3,128,384]{2,1,0:T(8,128)(2,1)S(1)}, u32[]{:S(2)}, u32[]{:S(2)}) collective-permute-start(bf16[3,128,384]{2,1,0:T(8,128)(2,1)S(1)} %shard_map.47.refs_0_), channel_id=1, source_target_pairs={{0,4},{1,5},{2,6},{3,7},{4,8},{5,9},{6,10},{7,11},{8,12},{9,13},{1... | collective-permute-start | bytes 884744 | tf_op jit(solution)/shard_map/ppermute | solution.py:34
  10.1 3.3 %collective-permute-start.4 = (bf16[3,128,384]{2,1,0:T(8,128)(2,1)S(1)}, bf16[3,128,384]{2,1,0:T(8,128)(2,1)S(1)}, u32[]{:S(2)}, u32[]{:S(2)}) collective-permute-start(bf16[3,128,384]{2,1,0:T(8,128)(2,1)S(1)} %shard_map.47.refs_0_), channel_id=1, source_target_pairs={{0,8},{1,9},{2,10},{3,11},{4,12},{5,13},{6,14},{7,15},{8,0},{9,1},... | collective-permute-start | bytes 884744 | tf_op jit(solution)/shard_map/ppermute | solution.py:34
  13.4 0.7 collective-permute-start.5
  14.1 3.4 %collective-permute-done.3.refs_1_ = bf16[3,128,384]{2,1,0:T(8,128)(2,1)S(1)} collective-permute-done((bf16[3,128,384]{2,1,0:T(8,128)(2,1)S(1)}, bf16[3,128,384]{2,1,0:T(8,128)(2,1)S(1)}, u32[]{:S(2)}, u32[]{:S(2)}) %collective-permute-start.3) | collective-permute-done | bytes 294944 | tf_op jit(solution)/shard_map/ppermute | solution.py:34
  17.5 7.2 %collective-permute-done.4.refs_2_ = bf16[3,128,384]{2,1,0:T(8,128)(2,1)S(1)} collective-permute-done((bf16[3,128,384]{2,1,0:T(8,128)(2,1)S(1)}, bf16[3,128,384]{2,1,0:T(8,128)(2,1)S(1)}, u32[]{:S(2)}, u32[]{:S(2)}) %collective-permute-start.4) | collective-permute-done | bytes 294944 | tf_op jit(solution)/shard_map/ppermute | solution.py:34
  24.7 0.6 collective-permute-done.5.refs_3_
  25.3 0.1 shard_map.48.right_moved
  25.4 2.5 %collective-permute-start.6 = (bf16[12,128,384]{2,1,0:T(8,128)(2,1)S(1)}, bf16[12,128,384]{2,1,0:T(8,128)(2,1)S(1)}, u32[]{:S(2)}, u32[]{:S(2)}) collective-permute-start(bf16[12,128,384]{2,1,0:T(8,128)(2,1)S(1)} %shard_map.48.right_moved), channel_id=1, source_target_pairs={{0,1},{1,0},{2,3},{3,2},{4,5},{5,4},{6,7},{7,6},{8,9},{9,8},{10,11... | collective-permute-start | bytes 3538952 | tf_op jit(solution)/shard_map/ppermute | solution.py:34
  27.9 0.3 collective-permute-start.13
  28.2 0.2 copy.8
  28.4 0.1 fusion
  28.5 0.6 collective-permute-start.7
  29.1 1.0 collective-permute-start.11
  30.1 10.1 %collective-permute-done.13.moved = bf16[2,256,384]{2,1,0:T(8,128)(2,1)S(1)} collective-permute-done((bf16[2,256,384]{2,1,0:T(8,128)(2,1)S(1)}, bf16[2,256,384]{2,1,0:T(8,128)(2,1)S(1)}, u32[]{:S(2)}, u32[]{:S(2)}) %collective-permute-start.13) | collective-permute-done | bytes 393248 | tf_op jit(solution)/shard_map/ppermute | solution.py:34
  40.1 0.9 collective-permute-start.14
  41.0 1.0 collective-permute-start.8
  42.1 0.0 collective-permute-done.7.refs_5_
  42.1 0.4 collective-permute-start.9
  42.5 0.1 pad_add_fusion.place
  42.6 0.0 collective-permute-done.11.refs_6_
  42.6 1.3 collective-permute-start.10
  43.9 0.0 collective-permute-done.14.swapped
  43.9 0.5 collective-permute-start.12
  44.4 1.6 %shard_map.46.refs_0_ = bf16[1024,1024]{1,0:T(8,128)(2,1)S(1)} custom-call(bf16[4,256,384]{2,1,0:T(8,128)(2,1)S(1)} %copy-done, bf16[4,256,384]{2,1,0:T(8,128)(2,1)S(1)} %copy-done), custom_call_target="tpu_custom_call" | custom-call | flops 805306368 | bytes 1048576 | tf_op jit(solution)/shard_map/pallas_call | solution.py:75
  46.0 2.2 %shard_map.52.refs_0_ = bf16[1024,1024]{1,0:T(8,128)(2,1)S(1)} custom-call(s32[2]{0:T(128)S(1)} %pad_add_fusion.place, bf16[2,256,384]{2,1,0:T(8,128)(2,1)S(1)} %collective-permute-done.13.moved, bf16[2,256,384]{2,1,0:T(8,128)(2,1)S(1)} %collective-permute-done.14.swapped, bf16[4,256,384]{2,1,0:T(8,128)(2,1)S(1)} %copy-done), custom_call_target="tpu_custom_call" | custom-call | flops 805306368 | bytes 1048576 | tf_op jit(solution)/shard_map/pallas_call | solution.py:75
  48.2 0.0 collective-permute-done.6.right_swapped
  48.2 4.6 %shard_map.53.refs_1_.refs_2_.refs_3_ = bf16[1024,3072]{1,0:T(8,128)(2,1)S(1)} custom-call(s32[2]{0:T(128)S(1)} %pad_add_fusion.place, bf16[2,256,384]{2,1,0:T(8,128)(2,1)S(1)} %collective-permute-done.13.moved, bf16[2,256,384]{2,1,0:T(8,128)(2,1)S(1)} %collective-permute-done.14.swapped, bf16[12,128,384]{2,1,0:T(8,128)(2,1)S(1)} %shard_map.48.right_moved, ...), custom_call_target="tpu_custom_call" | custom-call | flops 2415919104 | bytes 1048576 | tf_op jit(solution)/shard_map/pallas_call | solution.py:75
  52.8 1.7 %collective-permute-done.8.refs_6_ = bf16[1024,256]{1,0:T(8,128)(2,1)S(1)} collective-permute-done((bf16[1024,256]{1,0:T(8,128)(2,1)S(1)}, bf16[1024,256]{1,0:T(8,128)(2,1)S(1)}, u32[]{:S(2)}, u32[]{:S(2)}) %collective-permute-start.8) | collective-permute-done | bytes 524320 | tf_op jit(solution)/shard_map/ppermute | solution.py:34
  54.5 0.6 collective-permute-done.9.refs_7_
  55.1 2.3 %shard_map.54 = bf16[1024,256]{1,0:T(8,128)(2,1)S(1)} custom-call(bf16[1024,1024]{1,0:T(8,128)(2,1)S(1)} %shard_map.52.refs_0_, bf16[1024,3072]{1,0:T(8,128)(2,1)S(1)} %shard_map.53.refs_1_.refs_2_.refs_3_, bf16[1024,3072]{1,0:T(8,128)(2,1)S(1)} %shard_map.53.refs_1_.refs_2_.refs_3_, bf16[1024,3072]{1,0:T(8,128)(2,1)S(1)} %shard_map.53.refs_1_.refs_2_.refs_3_, ...), custom_call_target="tpu_custom_call" | custom-call | flops 2147483648 | bytes 1048576 | tf_op jit(solution)/shard_map/pallas_call | solution.py:75
  57.5 2.8 %collective-permute-start.15 = (bf16[1024,256]{1,0:T(8,128)(2,1)S(1)}, bf16[1024,256]{1,0:T(8,128)(2,1)S(1)}, u32[]{:S(2)}, u32[]{:S(2)}) collective-permute-start(bf16[1024,256]{1,0:T(8,128)(2,1)S(1)} %shard_map.54), channel_id=1, source_target_pairs={{0,64},{1,65},{2,66},{3,67},{4,68},{5,69},{6,70},{7,71},{8,72},{9,... | collective-permute-start | bytes 1572872 | tf_op jit(solution)/shard_map/ppermute | solution.py:34
  60.3 6.1 %collective-permute-done.10.refs_5_ = bf16[1024,256]{1,0:T(8,128)(2,1)S(1)} collective-permute-done((bf16[1024,256]{1,0:T(8,128)(2,1)S(1)}, bf16[1024,256]{1,0:T(8,128)(2,1)S(1)}, u32[]{:S(2)}, u32[]{:S(2)}) %collective-permute-start.10) | collective-permute-done | bytes 524320 | tf_op jit(solution)/shard_map/ppermute | solution.py:34
  66.4 0.0 collective-permute-done.12.refs_7_
  66.4 2.3 %shard_map.55 = bf16[1024,256]{1,0:T(8,128)(2,1)S(1)} custom-call(bf16[1024,1024]{1,0:T(8,128)(2,1)S(1)} %shard_map.52.refs_0_, bf16[1024,3072]{1,0:T(8,128)(2,1)S(1)} %shard_map.53.refs_1_.refs_2_.refs_3_, bf16[1024,3072]{1,0:T(8,128)(2,1)S(1)} %shard_map.53.refs_1_.refs_2_.refs_3_, bf16[1024,3072]{1,0:T(8,128)(2,1)S(1)} %shard_map.53.refs_1_.refs_2_.refs_3_, ...), custom_call_target="tpu_custom_call" | custom-call | flops 2147483648 | bytes 1048576 | tf_op jit(solution)/shard_map/pallas_call | solution.py:75
  68.7 3.0 %collective-permute-start.16 = (bf16[1024,256]{1,0:T(8,128)(2,1)S(1)}, bf16[1024,256]{1,0:T(8,128)(2,1)S(1)}, u32[]{:S(2)}, u32[]{:S(2)}) collective-permute-start(bf16[1024,256]{1,0:T(8,128)(2,1)S(1)} %shard_map.55), channel_id=1, source_target_pairs={{0,64},{1,65},{2,66},{3,67},{4,68},{5,69},{6,70},{7,71},{8,72},{9,... | collective-permute-start | bytes 1572872 | tf_op jit(solution)/shard_map/ppermute | solution.py:34
  71.7 4.6 %shard_map.49.refs_1_.refs_2_.refs_3_ = bf16[1024,3072]{1,0:T(8,128)(2,1)S(1)} custom-call(s32[2]{0:T(128)S(1)} %pad_add_fusion.place, bf16[4,256,384]{2,1,0:T(8,128)(2,1)S(1)} %copy-done, bf16[12,128,384]{2,1,0:T(8,128)(2,1)S(1)} %shard_map.48.right_moved, bf16[12,128,384]{2,1,0:T(8,128)(2,1)S(1)} %collective-permute-done.6.right_swapped), custom_call_target="tpu_custom_call" | custom-call | flops 2415919104 | bytes 1048576 | tf_op jit(solution)/shard_map/pallas_call | solution.py:75
  76.3 2.3 %shard_map.50.refs_0_.mine = f32[1024,256]{1,0:T(8,128)S(1)} custom-call(bf16[1024,1024]{1,0:T(8,128)(2,1)S(1)} %shard_map.46.refs_0_, bf16[1024,3072]{1,0:T(8,128)(2,1)S(1)} %shard_map.49.refs_1_.refs_2_.refs_3_, bf16[1024,3072]{1,0:T(8,128)(2,1)S(1)} %shard_map.49.refs_1_.refs_2_.refs_3_, bf16[1024,3072]{1,0:T(8,128)(2,1)S(1)} %shard_map.49.refs_1_.refs_2_.refs_3_, ...), custom_call_target="tpu_custom_call" | custom-call | flops 2147483648 | bytes 1048576 | tf_op jit(solution)/shard_map/pallas_call | solution.py:75
  78.6 0.0 collective-permute-done.15.refs_2_.received
  78.7 0.9 round.2
  79.6 3.8 %collective-permute-start.17 = (bf16[1024,128]{1,0:T(8,128)(2,1)S(1)}, bf16[1024,128]{1,0:T(8,128)(2,1)S(1)}, u32[]{:S(2)}, u32[]{:S(2)}) collective-permute-start(bf16[1024,128]{1,0:T(8,128)(2,1)S(1)} %get-tuple-element.13), channel_id=1, source_target_pairs={{0,0},{1,1},{2,10},{3,11},{4,4},{5,5},{6,14},{7,15},{8,8},{9,9},{1... | collective-permute-start | bytes 786440 | tf_op jit(solution)/shard_map/ppermute | solution.py:34
  83.4 3.1 %collective-permute-start.18 = (bf16[1024,128]{1,0:T(8,128)(2,1)S(1)}, bf16[1024,128]{1,0:T(8,128)(2,1)S(1)}, u32[]{:S(2)}, u32[]{:S(2)}) collective-permute-start(bf16[1024,128]{1,0:T(8,128)(2,1)S(1)} %get-tuple-element.14), channel_id=1, source_target_pairs={{0,1},{1,0},{2,11},{3,10},{4,5},{5,4},{6,15},{7,14},{8,9},{9,8},{1... | collective-permute-start | bytes 786440 | tf_op jit(solution)/shard_map/ppermute | solution.py:34
  86.4 2.1 %collective-permute-done.17.refs_0_ = bf16[1024,128]{1,0:T(8,128)(2,1)S(1)} collective-permute-done((bf16[1024,128]{1,0:T(8,128)(2,1)S(1)}, bf16[1024,128]{1,0:T(8,128)(2,1)S(1)}, u32[]{:S(2)}, u32[]{:S(2)}) %collective-permute-start.17) | collective-permute-done | bytes 262176 | tf_op jit(solution)/shard_map/ppermute | solution.py:34
  88.5 7.8 %collective-permute-done.18.refs_1_ = bf16[1024,128]{1,0:T(8,128)(2,1)S(1)} collective-permute-done((bf16[1024,128]{1,0:T(8,128)(2,1)S(1)}, bf16[1024,128]{1,0:T(8,128)(2,1)S(1)}, u32[]{:S(2)}, u32[]{:S(2)}) %collective-permute-start.18) | collective-permute-done | bytes 262176 | tf_op jit(solution)/shard_map/ppermute | solution.py:34
  96.3 0.8 shard_map.56
  97.2 2.8 %collective-permute-start.19 = (bf16[2048,128]{1,0:T(8,128)(2,1)}, bf16[2048,128]{1,0:T(8,128)(2,1)}, u32[]{:S(2)}, u32[]{:S(2)}) collective-permute-start(bf16[2048,128]{1,0:T(8,128)(2,1)} %shard_map.56), channel_id=1, source_target_pairs={{0,0},{1,1},{2,80},{3,81},{4,32},{5,33},{6,112},{7,113},{8,64},{9,... | collective-permute-start | bytes 1572872 | tf_op jit(solution)/shard_map/ppermute | solution.py:34
  99.9 2.3 %shard_map.51.refs_1_.mine = f32[1024,256]{1,0:T(8,128)S(1)} custom-call(bf16[1024,1024]{1,0:T(8,128)(2,1)S(1)} %shard_map.46.refs_0_, bf16[1024,3072]{1,0:T(8,128)(2,1)S(1)} %shard_map.49.refs_1_.refs_2_.refs_3_, bf16[1024,3072]{1,0:T(8,128)(2,1)S(1)} %shard_map.49.refs_1_.refs_2_.refs_3_, bf16[1024,3072]{1,0:T(8,128)(2,1)S(1)} %shard_map.49.refs_1_.refs_2_.refs_3_, ...), custom_call_target="tpu_custom_call" | custom-call | flops 2147483648 | bytes 1048576 | tf_op jit(solution)/shard_map/pallas_call | solution.py:75
  102.3 0.0 collective-permute-done.16.refs_3_.received
  102.3 1.6 %round.3 = (bf16[1024,128]{1,0:T(8,128)(2,1)}, bf16[1024,128]{1,0:T(8,128)(2,1)}) custom-call(s32[2]{0:T(128)S(1)} %pad_add_fusion.place, f32[1024,256]{1,0:T(8,128)S(1)} %shard_map.51.refs_1_.mine, bf16[1024,256]{1,0:T(8,128)(2,1)S(1)} %collective-permute-done.16.refs_3_.received), custom_call_target="tpu_custom_call" | custom-call | flops 262144 | bytes 1572864 | tf_op jit(solution)/shard_map/round/pallas_call | solution.py:196
  103.9 5.5 %collective-permute-start.20 = (bf16[1024,128]{1,0:T(8,128)(2,1)}, bf16[1024,128]{1,0:T(8,128)(2,1)S(1)}, u32[]{:S(2)}, u32[]{:S(2)}) collective-permute-start(bf16[1024,128]{1,0:T(8,128)(2,1)} %get-tuple-element.15), channel_id=1, source_target_pairs={{0,0},{1,1},{2,16},{3,17},{4,32},{5,33},{6,48},{7,49},{8,64},{9,65... | collective-permute-start | bytes 786440 | tf_op jit(solution)/shard_map/ppermute | solution.py:34
  109.4 0.9 collective-permute-start.21
  110.4 0.1 dynamic_slice.12.occ_first
  110.4 0.1 dynamic_slice.13.occ_second
  110.5 0.1 copy.6.vir_col
  110.7 1.1 prepare.1
  111.7 23.1 %collective-permute-done.20.late_same = bf16[1024,128]{1,0:T(8,128)(2,1)S(1)} collective-permute-done((bf16[1024,128]{1,0:T(8,128)(2,1)}, bf16[1024,128]{1,0:T(8,128)(2,1)S(1)}, u32[]{:S(2)}, u32[]{:S(2)}) %collective-permute-start.20) | collective-permute-done | bytes 262176 | tf_op jit(solution)/shard_map/ppermute | solution.py:34
  134.9 5.7 %collective-permute-done.21.late_other = bf16[1024,128]{1,0:T(8,128)(2,1)} collective-permute-done((bf16[1024,128]{1,0:T(8,128)(2,1)}, bf16[1024,128]{1,0:T(8,128)(2,1)}, u32[]{:S(2)}, u32[]{:S(2)}) %collective-permute-start.21) | collective-permute-done | bytes 262176 | tf_op jit(solution)/shard_map/ppermute | solution.py:34
  140.6 3.6 %finish.1 = f32[4096,128]{1,0:T(8,128)} custom-call(s32[2]{0:T(128)S(1)} %pad_add_fusion.place, f32[4096,128]{1,0:T(8,128)S(1)} %get-tuple-element.11.base, f32[4096,128]{1,0:T(8,128)S(1)} %get-tuple-element.12.inverse, bf16[2048,128]{1,0:T(8,128)(2,1)} %collective-permute-done.19.early_both, bf16[1024,128]{1,0:T(8,128)(2,1)S(1)} %collective-permute-done.20.late_same, ...), custom_call_target="tpu_custom_call" | custom-call | flops 1048576 | bytes 6291456 | tf_op jit(solution)/shard_map/finish/pallas_call | solution.py:322
  (11 shorter events, 0.1 us)
Async XLA Ops:
  0.0 27.9 %copy-start = (bf16[4,256,384]{2,1,0:T(8,128)(2,1)S(1)}, bf16[4,256,384]{2,1,0:T(8,128)(2,1)}, u32[]{:S(2)}) copy-start(bf16[4,256,384]{2,1,0:T(8,128)(2,1)} %right.3) | copy-start | bytes 2359300
  0.0 28.2 %copy-start.2 = (bf16[4,256,2,256]{3,2,1,0:T(2,128)(2,1)S(1)}, bf16[4,256,2,256]{3,2,1,0:T(2,128)(2,1)}, u32[]{:S(2)}) copy-start(bf16[4,256,2,256]{3,2,1,0:T(2,128)(2,1)} %param.4) | copy-start | bytes 3145732
  1.0 3.6 %collective-permute-start = (bf16[1,128,384]{2,1,0:T(8,128)(2,1)S(1)}, bf16[1,128,384]{2,1,0:T(8,128)(2,1)S(1)}, u32[]{:S(2)}, u32[]{:S(2)}) collective-permute-start(bf16[1,128,384]{2,1,0:T(8,128)(2,1)S(1)} %constant_dynamic-slice_fusion.1), channel_id=1, source_target_pairs={{0,16},{1,17},{2,18},{3,19},{4,20},{5,21},{6,22},{7,23},{8,24},{9,... | collective-permute-start | bytes 294920 | tf_op jit(solution)/shard_map/ppermute | solution.py:34
  2.4 3.6 %collective-permute-start.1 = (bf16[1,128,384]{2,1,0:T(8,128)(2,1)S(1)}, bf16[1,128,384]{2,1,0:T(8,128)(2,1)S(1)}, u32[]{:S(2)}, u32[]{:S(2)}) collective-permute-start(bf16[1,128,384]{2,1,0:T(8,128)(2,1)S(1)} %constant_dynamic-slice_fusion.1), channel_id=1, source_target_pairs={{0,48},{1,49},{2,50},{3,51},{4,52},{5,53},{6,54},{7,55},{8,56},{9,... | collective-permute-start | bytes 294920 | tf_op jit(solution)/shard_map/ppermute | solution.py:34
  2.6 5.8 %collective-permute-start.2 = (bf16[1,128,384]{2,1,0:T(8,128)(2,1)S(1)}, bf16[1,128,384]{2,1,0:T(8,128)(2,1)S(1)}, u32[]{:S(2)}, u32[]{:S(2)}) collective-permute-start(bf16[1,128,384]{2,1,0:T(8,128)(2,1)S(1)} %constant_dynamic-slice_fusion.1), channel_id=1, source_target_pairs={{0,32},{1,33},{2,34},{3,35},{4,36},{5,37},{6,38},{7,39},{8,40},{9,... | collective-permute-start | bytes 294920 | tf_op jit(solution)/shard_map/ppermute | solution.py:34
  8.4 9.1 %collective-permute-start.3 = (bf16[3,128,384]{2,1,0:T(8,128)(2,1)S(1)}, bf16[3,128,384]{2,1,0:T(8,128)(2,1)S(1)}, u32[]{:S(2)}, u32[]{:S(2)}) collective-permute-start(bf16[3,128,384]{2,1,0:T(8,128)(2,1)S(1)} %shard_map.47.refs_0_), channel_id=1, source_target_pairs={{0,4},{1,5},{2,6},{3,7},{4,8},{5,9},{6,10},{7,11},{8,12},{9,13},{1... | collective-permute-start | bytes 884744 | tf_op jit(solution)/shard_map/ppermute | solution.py:34
  10.1 14.6 %collective-permute-start.4 = (bf16[3,128,384]{2,1,0:T(8,128)(2,1)S(1)}, bf16[3,128,384]{2,1,0:T(8,128)(2,1)S(1)}, u32[]{:S(2)}, u32[]{:S(2)}) collective-permute-start(bf16[3,128,384]{2,1,0:T(8,128)(2,1)S(1)} %shard_map.47.refs_0_), channel_id=1, source_target_pairs={{0,8},{1,9},{2,10},{3,11},{4,12},{5,13},{6,14},{7,15},{8,0},{9,1},... | collective-permute-start | bytes 884744 | tf_op jit(solution)/shard_map/ppermute | solution.py:34
  13.4 11.9 %collective-permute-start.5 = (bf16[3,128,384]{2,1,0:T(8,128)(2,1)S(1)}, bf16[3,128,384]{2,1,0:T(8,128)(2,1)S(1)}, u32[]{:S(2)}, u32[]{:S(2)}) collective-permute-start(bf16[3,128,384]{2,1,0:T(8,128)(2,1)S(1)} %shard_map.47.refs_0_), channel_id=1, source_target_pairs={{0,12},{1,13},{2,14},{3,15},{4,0},{5,1},{6,2},{7,3},{8,4},{9,5},{1... | collective-permute-start | bytes 884744 | tf_op jit(solution)/shard_map/ppermute | solution.py:34
  25.4 22.8 %collective-permute-start.6 = (bf16[12,128,384]{2,1,0:T(8,128)(2,1)S(1)}, bf16[12,128,384]{2,1,0:T(8,128)(2,1)S(1)}, u32[]{:S(2)}, u32[]{:S(2)}) collective-permute-start(bf16[12,128,384]{2,1,0:T(8,128)(2,1)S(1)} %shard_map.48.right_moved), channel_id=1, source_target_pairs={{0,1},{1,0},{2,3},{3,2},{4,5},{5,4},{6,7},{7,6},{8,9},{9,8},{10,11... | collective-permute-start | bytes 3538952 | tf_op jit(solution)/shard_map/ppermute | solution.py:34
  27.9 12.2 %collective-permute-start.13 = (bf16[2,256,384]{2,1,0:T(8,128)(2,1)S(1)}, bf16[2,256,384]{2,1,0:T(8,128)(2,1)S(1)}, u32[]{:S(2)}, u32[]{:S(2)}) collective-permute-start(bf16[2,256,384]{2,1,0:T(8,128)(2,1)S(1)} %constant_dynamic-slice_fusion), channel_id=1, source_target_pairs={{0,64},{1,65},{2,66},{3,67},{4,68},{5,69},{6,70},{7,71},{8,72},{9,... | collective-permute-start | bytes 1179656 | tf_op jit(solution)/shard_map/ppermute | solution.py:34
  28.5 13.5 %collective-permute-start.7 = (bf16[1024,256]{1,0:T(8,128)(2,1)S(1)}, bf16[1024,256]{1,0:T(8,128)(2,1)S(1)}, u32[]{:S(2)}, u32[]{:S(2)}) collective-permute-start(bf16[1024,256]{1,0:T(8,128)(2,1)S(1)} %get-tuple-element.18.refs_4_), channel_id=1, source_target_pairs={{0,16},{1,17},{2,18},{3,19},{4,20},{5,21},{6,22},{7,23},{8,24},{9,... | collective-permute-start | bytes 1572872 | tf_op jit(solution)/shard_map/ppermute | solution.py:34
  29.1 13.5 %collective-permute-start.11 = (bf16[1024,256]{1,0:T(8,128)(2,1)S(1)}, bf16[1024,256]{1,0:T(8,128)(2,1)S(1)}, u32[]{:S(2)}, u32[]{:S(2)}) collective-permute-start(bf16[1024,256]{1,0:T(8,128)(2,1)S(1)} %get-tuple-element.17.refs_4_), channel_id=1, source_target_pairs={{0,48},{1,49},{2,50},{3,51},{4,52},{5,53},{6,54},{7,55},{8,56},{9,... | collective-permute-start | bytes 1572872 | tf_op jit(solution)/shard_map/ppermute | solution.py:34
  40.1 3.8 %collective-permute-start.14 = (bf16[2,256,384]{2,1,0:T(8,128)(2,1)S(1)}, bf16[2,256,384]{2,1,0:T(8,128)(2,1)S(1)}, u32[]{:S(2)}, u32[]{:S(2)}) collective-permute-start(bf16[2,256,384]{2,1,0:T(8,128)(2,1)S(1)} %collective-permute-done.13.moved), channel_id=1, source_target_pairs={{0,1},{1,0},{2,3},{3,2},{4,5},{5,4},{6,7},{7,6},{8,9},{9,8},{10,11... | collective-permute-start | bytes 1179656 | tf_op jit(solution)/shard_map/ppermute | solution.py:34
  41.0 13.5 %collective-permute-start.8 = (bf16[1024,256]{1,0:T(8,128)(2,1)S(1)}, bf16[1024,256]{1,0:T(8,128)(2,1)S(1)}, u32[]{:S(2)}, u32[]{:S(2)}) collective-permute-start(bf16[1024,256]{1,0:T(8,128)(2,1)S(1)} %get-tuple-element.18.refs_4_), channel_id=1, source_target_pairs={{0,48},{1,49},{2,50},{3,51},{4,52},{5,53},{6,54},{7,55},{8,56},{9,... | collective-permute-start | bytes 1572872 | tf_op jit(solution)/shard_map/ppermute | solution.py:34
  42.1 13.1 %collective-permute-start.9 = (bf16[1024,256]{1,0:T(8,128)(2,1)S(1)}, bf16[1024,256]{1,0:T(8,128)(2,1)S(1)}, u32[]{:S(2)}, u32[]{:S(2)}) collective-permute-start(bf16[1024,256]{1,0:T(8,128)(2,1)S(1)} %collective-permute-done.7.refs_5_), channel_id=1, source_target_pairs={{0,16},{1,17},{2,18},{3,19},{4,20},{5,21},{6,22},{7,23},{8,24},{9,... | collective-permute-start | bytes 1572872 | tf_op jit(solution)/shard_map/ppermute | solution.py:34
  42.6 23.8 %collective-permute-start.10 = (bf16[1024,256]{1,0:T(8,128)(2,1)S(1)}, bf16[1024,256]{1,0:T(8,128)(2,1)S(1)}, u32[]{:S(2)}, u32[]{:S(2)}) collective-permute-start(bf16[1024,256]{1,0:T(8,128)(2,1)S(1)} %get-tuple-element.17.refs_4_), channel_id=1, source_target_pairs={{0,16},{1,17},{2,18},{3,19},{4,20},{5,21},{6,22},{7,23},{8,24},{9,... | collective-permute-start | bytes 1572872 | tf_op jit(solution)/shard_map/ppermute | solution.py:34
  43.9 22.5 %collective-permute-start.12 = (bf16[1024,256]{1,0:T(8,128)(2,1)S(1)}, bf16[1024,256]{1,0:T(8,128)(2,1)S(1)}, u32[]{:S(2)}, u32[]{:S(2)}) collective-permute-start(bf16[1024,256]{1,0:T(8,128)(2,1)S(1)} %collective-permute-done.11.refs_6_), channel_id=1, source_target_pairs={{0,48},{1,49},{2,50},{3,51},{4,52},{5,53},{6,54},{7,55},{8,56},{9,... | collective-permute-start | bytes 1572872 | tf_op jit(solution)/shard_map/ppermute | solution.py:34
  57.5 21.2 %collective-permute-start.15 = (bf16[1024,256]{1,0:T(8,128)(2,1)S(1)}, bf16[1024,256]{1,0:T(8,128)(2,1)S(1)}, u32[]{:S(2)}, u32[]{:S(2)}) collective-permute-start(bf16[1024,256]{1,0:T(8,128)(2,1)S(1)} %shard_map.54), channel_id=1, source_target_pairs={{0,64},{1,65},{2,66},{3,67},{4,68},{5,69},{6,70},{7,71},{8,72},{9,... | collective-permute-start | bytes 1572872 | tf_op jit(solution)/shard_map/ppermute | solution.py:34
  68.7 33.6 %collective-permute-start.16 = (bf16[1024,256]{1,0:T(8,128)(2,1)S(1)}, bf16[1024,256]{1,0:T(8,128)(2,1)S(1)}, u32[]{:S(2)}, u32[]{:S(2)}) collective-permute-start(bf16[1024,256]{1,0:T(8,128)(2,1)S(1)} %shard_map.55), channel_id=1, source_target_pairs={{0,64},{1,65},{2,66},{3,67},{4,68},{5,69},{6,70},{7,71},{8,72},{9,... | collective-permute-start | bytes 1572872 | tf_op jit(solution)/shard_map/ppermute | solution.py:34
  79.6 8.9 %collective-permute-start.17 = (bf16[1024,128]{1,0:T(8,128)(2,1)S(1)}, bf16[1024,128]{1,0:T(8,128)(2,1)S(1)}, u32[]{:S(2)}, u32[]{:S(2)}) collective-permute-start(bf16[1024,128]{1,0:T(8,128)(2,1)S(1)} %get-tuple-element.13), channel_id=1, source_target_pairs={{0,0},{1,1},{2,10},{3,11},{4,4},{5,5},{6,14},{7,15},{8,8},{9,9},{1... | collective-permute-start | bytes 786440 | tf_op jit(solution)/shard_map/ppermute | solution.py:34
  83.4 13.0 %collective-permute-start.18 = (bf16[1024,128]{1,0:T(8,128)(2,1)S(1)}, bf16[1024,128]{1,0:T(8,128)(2,1)S(1)}, u32[]{:S(2)}, u32[]{:S(2)}) collective-permute-start(bf16[1024,128]{1,0:T(8,128)(2,1)S(1)} %get-tuple-element.14), channel_id=1, source_target_pairs={{0,1},{1,0},{2,11},{3,10},{4,5},{5,4},{6,15},{7,14},{8,9},{9,8},{1... | collective-permute-start | bytes 786440 | tf_op jit(solution)/shard_map/ppermute | solution.py:34
  97.2 13.2 %copy-start.3 = (f32[32]{0:T(128)S(1)}, f32[32]{0:T(128)}, u32[]{:S(2)}) copy-start(f32[32]{0:T(128)} %param.6) | copy-start | bytes 388
  97.2 13.4 %copy-start.1 = (f32[256]{0:T(256)S(1)}, f32[256]{0:T(256)}, u32[]{:S(2)}) copy-start(f32[256]{0:T(256)} %param.7) | copy-start | bytes 3076
  97.2 43.4 %collective-permute-start.19 = (bf16[2048,128]{1,0:T(8,128)(2,1)}, bf16[2048,128]{1,0:T(8,128)(2,1)}, u32[]{:S(2)}, u32[]{:S(2)}) collective-permute-start(bf16[2048,128]{1,0:T(8,128)(2,1)} %shard_map.56), channel_id=1, source_target_pairs={{0,0},{1,1},{2,80},{3,81},{4,32},{5,33},{6,112},{7,113},{8,64},{9,... | collective-permute-start | bytes 1572872 | tf_op jit(solution)/shard_map/ppermute | solution.py:34
  103.9 31.0 %collective-permute-start.20 = (bf16[1024,128]{1,0:T(8,128)(2,1)}, bf16[1024,128]{1,0:T(8,128)(2,1)S(1)}, u32[]{:S(2)}, u32[]{:S(2)}) collective-permute-start(bf16[1024,128]{1,0:T(8,128)(2,1)} %get-tuple-element.15), channel_id=1, source_target_pairs={{0,0},{1,1},{2,16},{3,17},{4,32},{5,33},{6,48},{7,49},{8,64},{9,65... | collective-permute-start | bytes 786440 | tf_op jit(solution)/shard_map/ppermute | solution.py:34
  109.4 31.2 %collective-permute-start.21 = (bf16[1024,128]{1,0:T(8,128)(2,1)}, bf16[1024,128]{1,0:T(8,128)(2,1)}, u32[]{:S(2)}, u32[]{:S(2)}) collective-permute-start(bf16[1024,128]{1,0:T(8,128)(2,1)} %get-tuple-element.16), channel_id=1, source_target_pairs={{0,1},{1,0},{2,17},{3,16},{4,33},{5,32},{6,49},{7,48},{8,65},{9,64... | collective-permute-start | bytes 786440 | tf_op jit(solution)/shard_map/ppermute | solution.py:34
where the time goes:
time: 145 us; the launch traced here: 144 us
  waiting for transfers between devices  72.2 us (50%)
  starting transfers between devices  39.7 us (27%)
  Pallas kernels  30.4 us (21%)
  local copies, waits for them, and re-layouts  1.66 us (1%)
    ppermute x22, waiting for transfers between devices, send(): return lax.ppermute(value, AXES, permutation(move))  72.2 us
    ppermute x22, starting transfers between devices, send(): return lax.ppermute(value, AXES, permutation(move))  39.7 us
    pallas_call x11, Pallas kernels, call(): pl.pallas_call(kernel, out_shape=out_shape, in_specs=specs or [VMEM] * le...  23.2 us
    pallas_call x1, Pallas kernels, inner(): pl.pallas_call(final_kernel, out_shape=shape, grid_spec=pltpu.PrefetchSca...  3.61 us
  transfers between devices with their start and end apart: 22, of which 13 were waited for; matrix products, arithmetic and copies ran while one was open for 0% of the time, Pallas kernels for 18%

commit v1 on v0

--- a/solution.py
+++ b/solution.py
@@ -220,24 +220,22 @@
 
 
 def final_kernel(place, base, inverse, early_both, late_same, late_other, out):
-    size = out.shape[0]
-    early_same, early_other = early_both.at[:size], early_both.at[size:]
-    step = pl.program_id(0)
-    early = step < 2
-    same = place[0] == lax.rem(step, 2)
-
-    def finish(mirrored):
-        out[...] = base[...] + mirrored[...].astype(F32) * inverse[...]
-
-    for ref, first, own in (
-        (early_same, True, True),
-        (early_other, True, False),
-        (late_same, False, True),
-        (late_other, False, False),
-    ):
-        @pl.when((early == first) & (same == own))
+    size = late_same.shape[0]
+    for orbital in range(out.shape[0] // size):
+        rows = slice(orbital * size, (orbital + 1) * size)
+        same = place[0] == orbital // 2
+        if orbital % 2 == 0:
+            first = pl.ds(pl.multiple_of(jnp.where(same, 0, size), size), size)
+            out[rows, :] = base[rows, :] + early_both[first, :].astype(F32) * inverse[rows, :]
+            continue
+
+        @pl.when(same)
         def _():
-            finish(ref)
+            out[rows, :] = base[rows, :] + late_same[...].astype(F32) * inverse[rows, :]
+
+        @pl.when(jnp.logical_not(same))
+        def _():
+            out[rows, :] = base[rows, :] + late_other[...].astype(F32) * inverse[rows, :]
 
 
 def inner(amplitudes, factors, occ_energy, vir_energy):
@@ -313,25 +311,9 @@
         cost_estimate=pl.CostEstimate(flops=4 * shape.size, bytes_accessed=10 * shape.size, transcendentals=0),
         name="prepare",
     )(occ_first, occ_second, *operands)
-    block = shape.shape[0] // own_rows
-
-    def orbital_of(step, place):
-        return (lax.rem(step, 2) * 2 + step // 2, 0)
-
-    by_orbital = pl.BlockSpec((block, lanes), orbital_of)
-    out = pl.pallas_call(
-        final_kernel,
-        out_shape=shape,
-        grid_spec=pltpu.PrefetchScalarGridSpec(
-            num_scalar_prefetch=1,
-            grid=(own_rows,),
-            in_specs=[by_orbital] * 2 + [pl.BlockSpec(m.shape, lambda step, place: (0, 0)) for m in mirrored],
-            out_specs=by_orbital,
-        ),
-        compiler_params=pltpu.CompilerParams(vmem_limit_bytes=12 << 20),
-        cost_estimate=pl.CostEstimate(flops=2 * shape.size, bytes_accessed=12 * shape.size, transcendentals=0),
-        name="finish",
-    )(place, base, inverse, *mirrored)
+    operands = [place, base, inverse, *mirrored]
+    specs = [SMEM] + [VMEM] * (len(operands) - 1)
+    out = call(final_kernel, shape, operands, 2 * shape.size, specs=specs)
     out = out.reshape(own_rows, virtual, cuts, pairs_cols, lanes).transpose(0, 1, 3, 2, 4)
     return out.reshape(own_rows, virtual, pairs_cols, virtual)
 

time: 145 us -> 144 us (level)
    pallas_call x1 -> x0, Pallas kernels: 3.61 us -> none  [inner(): pl.pallas_call(final_kernel, out_shape=shape, grid_spec=pltpu.PrefetchSca...]
    pallas_call x11 -> x12, Pallas kernels: 23.2 us -> 25.9 us  [call(): pl.pallas_call(kernel, out_shape=out_shape, in_specs=specs or [VMEM] * le...]
  transfers between devices with their start and end apart: 22 -> 22, of which waited for: 13 -> 13; matrix products, arithmetic and copies ran while one was open for 0% -> 0% of each run, Pallas kernels for 18% -> 19%
where the time goes in v1:
time: 144 us; the launch traced here: 143 us
  waiting for transfers between devices  72.2 us (50%)
  starting transfers between devices  39.7 us (28%)
  Pallas kernels  29.5 us (20%)
  local copies, waits for them, and re-layouts  1.66 us (1%)
    ppermute x22, waiting for transfers between devices, send(): return lax.ppermute(value, AXES, permutation(move))  72.2 us
    ppermute x22, starting transfers between devices, send(): return lax.ppermute(value, AXES, permutation(move))  39.7 us
    pallas_call x12, Pallas kernels, call(): pl.pallas_call(kernel, out_shape=out_shape, in_specs=specs or [VMEM] * le...  25.9 us
  transfers between devices with their start and end apart: 22, of which 13 were waited for; matrix products, arithmetic and copies ran while one was open for 0% of the time, Pallas kernels for 19%

profile of v1, /device:TPU:13, one launch (start us, length us, event | category | flops | bytes accessed | tf_op | source)
XLA Modules:
  0.0 143.4 jit_solution(14133270126181728624)
XLA Ops:
  0.0 1.0 constant_dynamic-slice_fusion.1
  1.0 1.4 collective-permute-start
  2.4 0.2 collective-permute-start.1
  2.6 2.0 %collective-permute-start.2 = (bf16[1,128,384]{2,1,0:T(8,128)(2,1)S(1)}, bf16[1,128,384]{2,1,0:T(8,128)(2,1)S(1)}, u32[]{:S(2)}, u32[]{:S(2)}) collective-permute-start(bf16[1,128,384]{2,1,0:T(8,128)(2,1)S(1)} %constant_dynamic-slice_fusion.1), channel_id=1, source_target_pairs={{0,32},{1,33},{2,34},{3,35},{4,36},{5,37},{6,38},{7,39},{8,40},{9,... | collective-permute-start | bytes 294920 | tf_op jit(solution)/shard_map/ppermute | solution.py:34
  4.6 0.0 collective-permute-done.refs_0_
  4.6 1.4 collective-permute-done.1.refs_1_
  6.0 2.3 %collective-permute-done.2.refs_2_ = bf16[1,128,384]{2,1,0:T(8,128)(2,1)S(1)} collective-permute-done((bf16[1,128,384]{2,1,0:T(8,128)(2,1)S(1)}, bf16[1,128,384]{2,1,0:T(8,128)(2,1)S(1)}, u32[]{:S(2)}, u32[]{:S(2)}) %collective-permute-start.2) | collective-permute-done | bytes 98336 | tf_op jit(solution)/shard_map/ppermute | solution.py:34
  8.4 1.7 %collective-permute-start.3 = (bf16[3,128,384]{2,1,0:T(8,128)(2,1)S(1)}, bf16[3,128,384]{2,1,0:T(8,128)(2,1)S(1)}, u32[]{:S(2)}, u32[]{:S(2)}) collective-permute-start(bf16[3,128,384]{2,1,0:T(8,128)(2,1)S(1)} %shard_map.47.refs_0_), channel_id=1, source_target_pairs={{0,4},{1,5},{2,6},{3,7},{4,8},{5,9},{6,10},{7,11},{8,12},{9,13},{1... | collective-permute-start | bytes 884744 | tf_op jit(solution)/shard_map/ppermute | solution.py:34
  10.1 3.3 %collective-permute-start.4 = (bf16[3,128,384]{2,1,0:T(8,128)(2,1)S(1)}, bf16[3,128,384]{2,1,0:T(8,128)(2,1)S(1)}, u32[]{:S(2)}, u32[]{:S(2)}) collective-permute-start(bf16[3,128,384]{2,1,0:T(8,128)(2,1)S(1)} %shard_map.47.refs_0_), channel_id=1, source_target_pairs={{0,8},{1,9},{2,10},{3,11},{4,12},{5,13},{6,14},{7,15},{8,0},{9,1},... | collective-permute-start | bytes 884744 | tf_op jit(solution)/shard_map/ppermute | solution.py:34
  13.4 0.7 collective-permute-start.5
  14.1 3.4 %collective-permute-done.3.refs_1_ = bf16[3,128,384]{2,1,0:T(8,128)(2,1)S(1)} collective-permute-done((bf16[3,128,384]{2,1,0:T(8,128)(2,1)S(1)}, bf16[3,128,384]{2,1,0:T(8,128)(2,1)S(1)}, u32[]{:S(2)}, u32[]{:S(2)}) %collective-permute-start.3) | collective-permute-done | bytes 294944 | tf_op jit(solution)/shard_map/ppermute | solution.py:34
  17.5 7.2 %collective-permute-done.4.refs_2_ = bf16[3,128,384]{2,1,0:T(8,128)(2,1)S(1)} collective-permute-done((bf16[3,128,384]{2,1,0:T(8,128)(2,1)S(1)}, bf16[3,128,384]{2,1,0:T(8,128)(2,1)S(1)}, u32[]{:S(2)}, u32[]{:S(2)}) %collective-permute-start.4) | collective-permute-done | bytes 294944 | tf_op jit(solution)/shard_map/ppermute | solution.py:34
  24.7 0.6 collective-permute-done.5.refs_3_
  25.3 0.1 shard_map.48.right_moved
  25.4 2.5 %collective-permute-start.6 = (bf16[12,128,384]{2,1,0:T(8,128)(2,1)S(1)}, bf16[12,128,384]{2,1,0:T(8,128)(2,1)S(1)}, u32[]{:S(2)}, u32[]{:S(2)}) collective-permute-start(bf16[12,128,384]{2,1,0:T(8,128)(2,1)S(1)} %shard_map.48.right_moved), channel_id=1, source_target_pairs={{0,1},{1,0},{2,3},{3,2},{4,5},{5,4},{6,7},{7,6},{8,9},{9,8},{10,11... | collective-permute-start | bytes 3538952 | tf_op jit(solution)/shard_map/ppermute | solution.py:34
  27.9 0.3 collective-permute-start.13
  28.2 0.2 copy.8
  28.4 0.1 fusion
  28.5 0.6 collective-permute-start.7
  29.1 1.0 collective-permute-start.11
  30.1 10.1 %collective-permute-done.13.moved = bf16[2,256,384]{2,1,0:T(8,128)(2,1)S(1)} collective-permute-done((bf16[2,256,384]{2,1,0:T(8,128)(2,1)S(1)}, bf16[2,256,384]{2,1,0:T(8,128)(2,1)S(1)}, u32[]{:S(2)}, u32[]{:S(2)}) %collective-permute-start.13) | collective-permute-done | bytes 393248 | tf_op jit(solution)/shard_map/ppermute | solution.py:34
  40.1 0.9 collective-permute-start.14
  41.0 1.0 collective-permute-start.8
  42.1 0.0 collective-permute-done.7.refs_5_
  42.1 0.4 collective-permute-start.9
  42.5 0.1 pad_add_fusion.place
  42.6 0.0 collective-permute-done.11.refs_6_
  42.6 1.3 collective-permute-start.10
  43.9 0.0 collective-permute-done.14.swapped
  43.9 0.5 collective-permute-start.12
  44.4 1.6 %shard_map.46.refs_0_ = bf16[1024,1024]{1,0:T(8,128)(2,1)S(1)} custom-call(bf16[4,256,384]{2,1,0:T(8,128)(2,1)S(1)} %copy-done, bf16[4,256,384]{2,1,0:T(8,128)(2,1)S(1)} %copy-done), custom_call_target="tpu_custom_call" | custom-call | flops 805306368 | bytes 1048576 | tf_op jit(solution)/shard_map/pallas_call | solution.py:75
  46.0 2.2 %shard_map.52.refs_0_ = bf16[1024,1024]{1,0:T(8,128)(2,1)S(1)} custom-call(s32[2]{0:T(128)S(1)} %pad_add_fusion.place, bf16[2,256,384]{2,1,0:T(8,128)(2,1)S(1)} %collective-permute-done.13.moved, bf16[2,256,384]{2,1,0:T(8,128)(2,1)S(1)} %collective-permute-done.14.swapped, bf16[4,256,384]{2,1,0:T(8,128)(2,1)S(1)} %copy-done), custom_call_target="tpu_custom_call" | custom-call | flops 805306368 | bytes 1048576 | tf_op jit(solution)/shard_map/pallas_call | solution.py:75
  48.2 0.0 collective-permute-done.6.right_swapped
  48.2 4.6 %shard_map.53.refs_1_.refs_2_.refs_3_ = bf16[1024,3072]{1,0:T(8,128)(2,1)S(1)} custom-call(s32[2]{0:T(128)S(1)} %pad_add_fusion.place, bf16[2,256,384]{2,1,0:T(8,128)(2,1)S(1)} %collective-permute-done.13.moved, bf16[2,256,384]{2,1,0:T(8,128)(2,1)S(1)} %collective-permute-done.14.swapped, bf16[12,128,384]{2,1,0:T(8,128)(2,1)S(1)} %shard_map.48.right_moved, ...), custom_call_target="tpu_custom_call" | custom-call | flops 2415919104 | bytes 1048576 | tf_op jit(solution)/shard_map/pallas_call | solution.py:75
  52.8 1.7 %collective-permute-done.8.refs_6_ = bf16[1024,256]{1,0:T(8,128)(2,1)S(1)} collective-permute-done((bf16[1024,256]{1,0:T(8,128)(2,1)S(1)}, bf16[1024,256]{1,0:T(8,128)(2,1)S(1)}, u32[]{:S(2)}, u32[]{:S(2)}) %collective-permute-start.8) | collective-permute-done | bytes 524320 | tf_op jit(solution)/shard_map/ppermute | solution.py:34
  54.5 0.6 collective-permute-done.9.refs_7_
  55.1 2.3 %shard_map.54 = bf16[1024,256]{1,0:T(8,128)(2,1)S(1)} custom-call(bf16[1024,1024]{1,0:T(8,128)(2,1)S(1)} %shard_map.52.refs_0_, bf16[1024,3072]{1,0:T(8,128)(2,1)S(1)} %shard_map.53.refs_1_.refs_2_.refs_3_, bf16[1024,3072]{1,0:T(8,128)(2,1)S(1)} %shard_map.53.refs_1_.refs_2_.refs_3_, bf16[1024,3072]{1,0:T(8,128)(2,1)S(1)} %shard_map.53.refs_1_.refs_2_.refs_3_, ...), custom_call_target="tpu_custom_call" | custom-call | flops 2147483648 | bytes 1048576 | tf_op jit(solution)/shard_map/pallas_call | solution.py:75
  57.5 2.8 %collective-permute-start.15 = (bf16[1024,256]{1,0:T(8,128)(2,1)S(1)}, bf16[1024,256]{1,0:T(8,128)(2,1)S(1)}, u32[]{:S(2)}, u32[]{:S(2)}) collective-permute-start(bf16[1024,256]{1,0:T(8,128)(2,1)S(1)} %shard_map.54), channel_id=1, source_target_pairs={{0,64},{1,65},{2,66},{3,67},{4,68},{5,69},{6,70},{7,71},{8,72},{9,... | collective-permute-start | bytes 1572872 | tf_op jit(solution)/shard_map/ppermute | solution.py:34
  60.3 6.1 %collective-permute-done.10.refs_5_ = bf16[1024,256]{1,0:T(8,128)(2,1)S(1)} collective-permute-done((bf16[1024,256]{1,0:T(8,128)(2,1)S(1)}, bf16[1024,256]{1,0:T(8,128)(2,1)S(1)}, u32[]{:S(2)}, u32[]{:S(2)}) %collective-permute-start.10) | collective-permute-done | bytes 524320 | tf_op jit(solution)/shard_map/ppermute | solution.py:34
  66.4 0.0 collective-permute-done.12.refs_7_
  66.4 2.3 %shard_map.55 = bf16[1024,256]{1,0:T(8,128)(2,1)S(1)} custom-call(bf16[1024,1024]{1,0:T(8,128)(2,1)S(1)} %shard_map.52.refs_0_, bf16[1024,3072]{1,0:T(8,128)(2,1)S(1)} %shard_map.53.refs_1_.refs_2_.refs_3_, bf16[1024,3072]{1,0:T(8,128)(2,1)S(1)} %shard_map.53.refs_1_.refs_2_.refs_3_, bf16[1024,3072]{1,0:T(8,128)(2,1)S(1)} %shard_map.53.refs_1_.refs_2_.refs_3_, ...), custom_call_target="tpu_custom_call" | custom-call | flops 2147483648 | bytes 1048576 | tf_op jit(solution)/shard_map/pallas_call | solution.py:75
  68.7 3.0 %collective-permute-start.16 = (bf16[1024,256]{1,0:T(8,128)(2,1)S(1)}, bf16[1024,256]{1,0:T(8,128)(2,1)S(1)}, u32[]{:S(2)}, u32[]{:S(2)}) collective-permute-start(bf16[1024,256]{1,0:T(8,128)(2,1)S(1)} %shard_map.55), channel_id=1, source_target_pairs={{0,64},{1,65},{2,66},{3,67},{4,68},{5,69},{6,70},{7,71},{8,72},{9,... | collective-permute-start | bytes 1572872 | tf_op jit(solution)/shard_map/ppermute | solution.py:34
  71.7 4.6 %shard_map.49.refs_1_.refs_2_.refs_3_ = bf16[1024,3072]{1,0:T(8,128)(2,1)S(1)} custom-call(s32[2]{0:T(128)S(1)} %pad_add_fusion.place, bf16[4,256,384]{2,1,0:T(8,128)(2,1)S(1)} %copy-done, bf16[12,128,384]{2,1,0:T(8,128)(2,1)S(1)} %shard_map.48.right_moved, bf16[12,128,384]{2,1,0:T(8,128)(2,1)S(1)} %collective-permute-done.6.right_swapped), custom_call_target="tpu_custom_call" | custom-call | flops 2415919104 | bytes 1048576 | tf_op jit(solution)/shard_map/pallas_call | solution.py:75
  76.3 2.3 %shard_map.50.refs_0_.mine = f32[1024,256]{1,0:T(8,128)S(1)} custom-call(bf16[1024,1024]{1,0:T(8,128)(2,1)S(1)} %shard_map.46.refs_0_, bf16[1024,3072]{1,0:T(8,128)(2,1)S(1)} %shard_map.49.refs_1_.refs_2_.refs_3_, bf16[1024,3072]{1,0:T(8,128)(2,1)S(1)} %shard_map.49.refs_1_.refs_2_.refs_3_, bf16[1024,3072]{1,0:T(8,128)(2,1)S(1)} %shard_map.49.refs_1_.refs_2_.refs_3_, ...), custom_call_target="tpu_custom_call" | custom-call | flops 2147483648 | bytes 1048576 | tf_op jit(solution)/shard_map/pallas_call | solution.py:75
  78.6 0.0 collective-permute-done.15.refs_2_.received
  78.7 0.9 round.2
  79.6 3.8 %collective-permute-start.17 = (bf16[1024,128]{1,0:T(8,128)(2,1)S(1)}, bf16[1024,128]{1,0:T(8,128)(2,1)S(1)}, u32[]{:S(2)}, u32[]{:S(2)}) collective-permute-start(bf16[1024,128]{1,0:T(8,128)(2,1)S(1)} %get-tuple-element.13), channel_id=1, source_target_pairs={{0,0},{1,1},{2,10},{3,11},{4,4},{5,5},{6,14},{7,15},{8,8},{9,9},{1... | collective-permute-start | bytes 786440 | tf_op jit(solution)/shard_map/ppermute | solution.py:34
  83.4 3.1 %collective-permute-start.18 = (bf16[1024,128]{1,0:T(8,128)(2,1)S(1)}, bf16[1024,128]{1,0:T(8,128)(2,1)S(1)}, u32[]{:S(2)}, u32[]{:S(2)}) collective-permute-start(bf16[1024,128]{1,0:T(8,128)(2,1)S(1)} %get-tuple-element.14), channel_id=1, source_target_pairs={{0,1},{1,0},{2,11},{3,10},{4,5},{5,4},{6,15},{7,14},{8,9},{9,8},{1... | collective-permute-start | bytes 786440 | tf_op jit(solution)/shard_map/ppermute | solution.py:34
  86.4 2.1 %collective-permute-done.17.refs_0_ = bf16[1024,128]{1,0:T(8,128)(2,1)S(1)} collective-permute-done((bf16[1024,128]{1,0:T(8,128)(2,1)S(1)}, bf16[1024,128]{1,0:T(8,128)(2,1)S(1)}, u32[]{:S(2)}, u32[]{:S(2)}) %collective-permute-start.17) | collective-permute-done | bytes 262176 | tf_op jit(solution)/shard_map/ppermute | solution.py:34
  88.5 7.8 %collective-permute-done.18.refs_1_ = bf16[1024,128]{1,0:T(8,128)(2,1)S(1)} collective-permute-done((bf16[1024,128]{1,0:T(8,128)(2,1)S(1)}, bf16[1024,128]{1,0:T(8,128)(2,1)S(1)}, u32[]{:S(2)}, u32[]{:S(2)}) %collective-permute-start.18) | collective-permute-done | bytes 262176 | tf_op jit(solution)/shard_map/ppermute | solution.py:34
  96.3 0.8 shard_map.56
  97.2 2.8 %collective-permute-start.19 = (bf16[2048,128]{1,0:T(8,128)(2,1)}, bf16[2048,128]{1,0:T(8,128)(2,1)}, u32[]{:S(2)}, u32[]{:S(2)}) collective-permute-start(bf16[2048,128]{1,0:T(8,128)(2,1)} %shard_map.56), channel_id=1, source_target_pairs={{0,0},{1,1},{2,80},{3,81},{4,32},{5,33},{6,112},{7,113},{8,64},{9,... | collective-permute-start | bytes 1572872 | tf_op jit(solution)/shard_map/ppermute | solution.py:34
  99.9 2.3 %shard_map.51.refs_1_.mine = f32[1024,256]{1,0:T(8,128)S(1)} custom-call(bf16[1024,1024]{1,0:T(8,128)(2,1)S(1)} %shard_map.46.refs_0_, bf16[1024,3072]{1,0:T(8,128)(2,1)S(1)} %shard_map.49.refs_1_.refs_2_.refs_3_, bf16[1024,3072]{1,0:T(8,128)(2,1)S(1)} %shard_map.49.refs_1_.refs_2_.refs_3_, bf16[1024,3072]{1,0:T(8,128)(2,1)S(1)} %shard_map.49.refs_1_.refs_2_.refs_3_, ...), custom_call_target="tpu_custom_call" | custom-call | flops 2147483648 | bytes 1048576 | tf_op jit(solution)/shard_map/pallas_call | solution.py:75
  102.3 0.0 collective-permute-done.16.refs_3_.received
  102.3 1.6 %round.3 = (bf16[1024,128]{1,0:T(8,128)(2,1)}, bf16[1024,128]{1,0:T(8,128)(2,1)}) custom-call(s32[2]{0:T(128)S(1)} %pad_add_fusion.place, f32[1024,256]{1,0:T(8,128)S(1)} %shard_map.51.refs_1_.mine, bf16[1024,256]{1,0:T(8,128)(2,1)S(1)} %collective-permute-done.16.refs_3_.received), custom_call_target="tpu_custom_call" | custom-call | flops 262144 | bytes 1572864 | tf_op jit(solution)/shard_map/round/pallas_call | solution.py:196
  103.9 5.5 %collective-permute-start.20 = (bf16[1024,128]{1,0:T(8,128)(2,1)}, bf16[1024,128]{1,0:T(8,128)(2,1)S(1)}, u32[]{:S(2)}, u32[]{:S(2)}) collective-permute-start(bf16[1024,128]{1,0:T(8,128)(2,1)} %get-tuple-element.15), channel_id=1, source_target_pairs={{0,0},{1,1},{2,16},{3,17},{4,32},{5,33},{6,48},{7,49},{8,64},{9,65... | collective-permute-start | bytes 786440 | tf_op jit(solution)/shard_map/ppermute | solution.py:34
  109.4 0.9 collective-permute-start.21
  110.4 0.1 dynamic_slice.12.occ_first
  110.4 0.1 dynamic_slice.13.occ_second
  110.5 0.1 copy.6.vir_col
  110.7 1.1 prepare.1
  111.7 23.1 %collective-permute-done.20.late_same = bf16[1024,128]{1,0:T(8,128)(2,1)S(1)} collective-permute-done((bf16[1024,128]{1,0:T(8,128)(2,1)}, bf16[1024,128]{1,0:T(8,128)(2,1)S(1)}, u32[]{:S(2)}, u32[]{:S(2)}) %collective-permute-start.20) | collective-permute-done | bytes 262176 | tf_op jit(solution)/shard_map/ppermute | solution.py:34
  134.9 5.7 %collective-permute-done.21.late_other = bf16[1024,128]{1,0:T(8,128)(2,1)} collective-permute-done((bf16[1024,128]{1,0:T(8,128)(2,1)}, bf16[1024,128]{1,0:T(8,128)(2,1)}, u32[]{:S(2)}, u32[]{:S(2)}) %collective-permute-start.21) | collective-permute-done | bytes 262176 | tf_op jit(solution)/shard_map/ppermute | solution.py:34
  140.6 2.8 %shard_map.57 = f32[4096,128]{1,0:T(8,128)} custom-call(s32[2]{0:T(128)S(1)} %pad_add_fusion.place, f32[4096,128]{1,0:T(8,128)S(1)} %get-tuple-element.11.base, f32[4096,128]{1,0:T(8,128)S(1)} %get-tuple-element.12.inverse, bf16[2048,128]{1,0:T(8,128)(2,1)} %collective-permute-done.19.early_both, bf16[1024,128]{1,0:T(8,128)(2,1)S(1)} %collective-permute-done.20.late_same, ...), custom_call_target="tpu_custom_call" | custom-call | flops 1048576 | bytes 1048576 | tf_op jit(solution)/shard_map/pallas_call | solution.py:75
  (11 shorter events, 0.1 us)
Async XLA Ops:
  0.0 27.9 %copy-start = (bf16[4,256,384]{2,1,0:T(8,128)(2,1)S(1)}, bf16[4,256,384]{2,1,0:T(8,128)(2,1)}, u32[]{:S(2)}) copy-start(bf16[4,256,384]{2,1,0:T(8,128)(2,1)} %right.3) | copy-start | bytes 2359300
  0.0 28.2 %copy-start.2 = (bf16[4,256,2,256]{3,2,1,0:T(2,128)(2,1)S(1)}, bf16[4,256,2,256]{3,2,1,0:T(2,128)(2,1)}, u32[]{:S(2)}) copy-start(bf16[4,256,2,256]{3,2,1,0:T(2,128)(2,1)} %param.4) | copy-start | bytes 3145732
  1.0 3.6 %collective-permute-start = (bf16[1,128,384]{2,1,0:T(8,128)(2,1)S(1)}, bf16[1,128,384]{2,1,0:T(8,128)(2,1)S(1)}, u32[]{:S(2)}, u32[]{:S(2)}) collective-permute-start(bf16[1,128,384]{2,1,0:T(8,128)(2,1)S(1)} %constant_dynamic-slice_fusion.1), channel_id=1, source_target_pairs={{0,16},{1,17},{2,18},{3,19},{4,20},{5,21},{6,22},{7,23},{8,24},{9,... | collective-permute-start | bytes 294920 | tf_op jit(solution)/shard_map/ppermute | solution.py:34
  2.4 3.6 %collective-permute-start.1 = (bf16[1,128,384]{2,1,0:T(8,128)(2,1)S(1)}, bf16[1,128,384]{2,1,0:T(8,128)(2,1)S(1)}, u32[]{:S(2)}, u32[]{:S(2)}) collective-permute-start(bf16[1,128,384]{2,1,0:T(8,128)(2,1)S(1)} %constant_dynamic-slice_fusion.1), channel_id=1, source_target_pairs={{0,48},{1,49},{2,50},{3,51},{4,52},{5,53},{6,54},{7,55},{8,56},{9,... | collective-permute-start | bytes 294920 | tf_op jit(solution)/shard_map/ppermute | solution.py:34
  2.6 5.8 %collective-permute-start.2 = (bf16[1,128,384]{2,1,0:T(8,128)(2,1)S(1)}, bf16[1,128,384]{2,1,0:T(8,128)(2,1)S(1)}, u32[]{:S(2)}, u32[]{:S(2)}) collective-permute-start(bf16[1,128,384]{2,1,0:T(8,128)(2,1)S(1)} %constant_dynamic-slice_fusion.1), channel_id=1, source_target_pairs={{0,32},{1,33},{2,34},{3,35},{4,36},{5,37},{6,38},{7,39},{8,40},{9,... | collective-permute-start | bytes 294920 | tf_op jit(solution)/shard_map/ppermute | solution.py:34
  8.4 9.1 %collective-permute-start.3 = (bf16[3,128,384]{2,1,0:T(8,128)(2,1)S(1)}, bf16[3,128,384]{2,1,0:T(8,128)(2,1)S(1)}, u32[]{:S(2)}, u32[]{:S(2)}) collective-permute-start(bf16[3,128,384]{2,1,0:T(8,128)(2,1)S(1)} %shard_map.47.refs_0_), channel_id=1, source_target_pairs={{0,4},{1,5},{2,6},{3,7},{4,8},{5,9},{6,10},{7,11},{8,12},{9,13},{1... | collective-permute-start | bytes 884744 | tf_op jit(solution)/shard_map/ppermute | solution.py:34
  10.1 14.6 %collective-permute-start.4 = (bf16[3,128,384]{2,1,0:T(8,128)(2,1)S(1)}, bf16[3,128,384]{2,1,0:T(8,128)(2,1)S(1)}, u32[]{:S(2)}, u32[]{:S(2)}) collective-permute-start(bf16[3,128,384]{2,1,0:T(8,128)(2,1)S(1)} %shard_map.47.refs_0_), channel_id=1, source_target_pairs={{0,8},{1,9},{2,10},{3,11},{4,12},{5,13},{6,14},{7,15},{8,0},{9,1},... | collective-permute-start | bytes 884744 | tf_op jit(solution)/shard_map/ppermute | solution.py:34
  13.4 11.9 %collective-permute-start.5 = (bf16[3,128,384]{2,1,0:T(8,128)(2,1)S(1)}, bf16[3,128,384]{2,1,0:T(8,128)(2,1)S(1)}, u32[]{:S(2)}, u32[]{:S(2)}) collective-permute-start(bf16[3,128,384]{2,1,0:T(8,128)(2,1)S(1)} %shard_map.47.refs_0_), channel_id=1, source_target_pairs={{0,12},{1,13},{2,14},{3,15},{4,0},{5,1},{6,2},{7,3},{8,4},{9,5},{1... | collective-permute-start | bytes 884744 | tf_op jit(solution)/shard_map/ppermute | solution.py:34
  25.4 22.8 %collective-permute-start.6 = (bf16[12,128,384]{2,1,0:T(8,128)(2,1)S(1)}, bf16[12,128,384]{2,1,0:T(8,128)(2,1)S(1)}, u32[]{:S(2)}, u32[]{:S(2)}) collective-permute-start(bf16[12,128,384]{2,1,0:T(8,128)(2,1)S(1)} %shard_map.48.right_moved), channel_id=1, source_target_pairs={{0,1},{1,0},{2,3},{3,2},{4,5},{5,4},{6,7},{7,6},{8,9},{9,8},{10,11... | collective-permute-start | bytes 3538952 | tf_op jit(solution)/shard_map/ppermute | solution.py:34
  27.9 12.2 %collective-permute-start.13 = (bf16[2,256,384]{2,1,0:T(8,128)(2,1)S(1)}, bf16[2,256,384]{2,1,0:T(8,128)(2,1)S(1)}, u32[]{:S(2)}, u32[]{:S(2)}) collective-permute-start(bf16[2,256,384]{2,1,0:T(8,128)(2,1)S(1)} %constant_dynamic-slice_fusion), channel_id=1, source_target_pairs={{0,64},{1,65},{2,66},{3,67},{4,68},{5,69},{6,70},{7,71},{8,72},{9,... | collective-permute-start | bytes 1179656 | tf_op jit(solution)/shard_map/ppermute | solution.py:34
  28.5 13.5 %collective-permute-start.7 = (bf16[1024,256]{1,0:T(8,128)(2,1)S(1)}, bf16[1024,256]{1,0:T(8,128)(2,1)S(1)}, u32[]{:S(2)}, u32[]{:S(2)}) collective-permute-start(bf16[1024,256]{1,0:T(8,128)(2,1)S(1)} %get-tuple-element.18.refs_4_), channel_id=1, source_target_pairs={{0,16},{1,17},{2,18},{3,19},{4,20},{5,21},{6,22},{7,23},{8,24},{9,... | collective-permute-start | bytes 1572872 | tf_op jit(solution)/shard_map/ppermute | solution.py:34
  29.1 13.5 %collective-permute-start.11 = (bf16[1024,256]{1,0:T(8,128)(2,1)S(1)}, bf16[1024,256]{1,0:T(8,128)(2,1)S(1)}, u32[]{:S(2)}, u32[]{:S(2)}) collective-permute-start(bf16[1024,256]{1,0:T(8,128)(2,1)S(1)} %get-tuple-element.17.refs_4_), channel_id=1, source_target_pairs={{0,48},{1,49},{2,50},{3,51},{4,52},{5,53},{6,54},{7,55},{8,56},{9,... | collective-permute-start | bytes 1572872 | tf_op jit(solution)/shard_map/ppermute | solution.py:34
  40.1 3.8 %collective-permute-start.14 = (bf16[2,256,384]{2,1,0:T(8,128)(2,1)S(1)}, bf16[2,256,384]{2,1,0:T(8,128)(2,1)S(1)}, u32[]{:S(2)}, u32[]{:S(2)}) collective-permute-start(bf16[2,256,384]{2,1,0:T(8,128)(2,1)S(1)} %collective-permute-done.13.moved), channel_id=1, source_target_pairs={{0,1},{1,0},{2,3},{3,2},{4,5},{5,4},{6,7},{7,6},{8,9},{9,8},{10,11... | collective-permute-start | bytes 1179656 | tf_op jit(solution)/shard_map/ppermute | solution.py:34
  41.0 13.5 %collective-permute-start.8 = (bf16[1024,256]{1,0:T(8,128)(2,1)S(1)}, bf16[1024,256]{1,0:T(8,128)(2,1)S(1)}, u32[]{:S(2)}, u32[]{:S(2)}) collective-permute-start(bf16[1024,256]{1,0:T(8,128)(2,1)S(1)} %get-tuple-element.18.refs_4_), channel_id=1, source_target_pairs={{0,48},{1,49},{2,50},{3,51},{4,52},{5,53},{6,54},{7,55},{8,56},{9,... | collective-permute-start | bytes 1572872 | tf_op jit(solution)/shard_map/ppermute | solution.py:34
  42.1 13.1 %collective-permute-start.9 = (bf16[1024,256]{1,0:T(8,128)(2,1)S(1)}, bf16[1024,256]{1,0:T(8,128)(2,1)S(1)}, u32[]{:S(2)}, u32[]{:S(2)}) collective-permute-start(bf16[1024,256]{1,0:T(8,128)(2,1)S(1)} %collective-permute-done.7.refs_5_), channel_id=1, source_target_pairs={{0,16},{1,17},{2,18},{3,19},{4,20},{5,21},{6,22},{7,23},{8,24},{9,... | collective-permute-start | bytes 1572872 | tf_op jit(solution)/shard_map/ppermute | solution.py:34
  42.6 23.8 %collective-permute-start.10 = (bf16[1024,256]{1,0:T(8,128)(2,1)S(1)}, bf16[1024,256]{1,0:T(8,128)(2,1)S(1)}, u32[]{:S(2)}, u32[]{:S(2)}) collective-permute-start(bf16[1024,256]{1,0:T(8,128)(2,1)S(1)} %get-tuple-element.17.refs_4_), channel_id=1, source_target_pairs={{0,16},{1,17},{2,18},{3,19},{4,20},{5,21},{6,22},{7,23},{8,24},{9,... | collective-permute-start | bytes 1572872 | tf_op jit(solution)/shard_map/ppermute | solution.py:34
  43.9 22.5 %collective-permute-start.12 = (bf16[1024,256]{1,0:T(8,128)(2,1)S(1)}, bf16[1024,256]{1,0:T(8,128)(2,1)S(1)}, u32[]{:S(2)}, u32[]{:S(2)}) collective-permute-start(bf16[1024,256]{1,0:T(8,128)(2,1)S(1)} %collective-permute-done.11.refs_6_), channel_id=1, source_target_pairs={{0,48},{1,49},{2,50},{3,51},{4,52},{5,53},{6,54},{7,55},{8,56},{9,... | collective-permute-start | bytes 1572872 | tf_op jit(solution)/shard_map/ppermute | solution.py:34
  57.5 21.2 %collective-permute-start.15 = (bf16[1024,256]{1,0:T(8,128)(2,1)S(1)}, bf16[1024,256]{1,0:T(8,128)(2,1)S(1)}, u32[]{:S(2)}, u32[]{:S(2)}) collective-permute-start(bf16[1024,256]{1,0:T(8,128)(2,1)S(1)} %shard_map.54), channel_id=1, source_target_pairs={{0,64},{1,65},{2,66},{3,67},{4,68},{5,69},{6,70},{7,71},{8,72},{9,... | collective-permute-start | bytes 1572872 | tf_op jit(solution)/shard_map/ppermute | solution.py:34
  68.7 33.6 %collective-permute-start.16 = (bf16[1024,256]{1,0:T(8,128)(2,1)S(1)}, bf16[1024,256]{1,0:T(8,128)(2,1)S(1)}, u32[]{:S(2)}, u32[]{:S(2)}) collective-permute-start(bf16[1024,256]{1,0:T(8,128)(2,1)S(1)} %shard_map.55), channel_id=1, source_target_pairs={{0,64},{1,65},{2,66},{3,67},{4,68},{5,69},{6,70},{7,71},{8,72},{9,... | collective-permute-start | bytes 1572872 | tf_op jit(solution)/shard_map/ppermute | solution.py:34
  79.6 8.9 %collective-permute-start.17 = (bf16[1024,128]{1,0:T(8,128)(2,1)S(1)}, bf16[1024,128]{1,0:T(8,128)(2,1)S(1)}, u32[]{:S(2)}, u32[]{:S(2)}) collective-permute-start(bf16[1024,128]{1,0:T(8,128)(2,1)S(1)} %get-tuple-element.13), channel_id=1, source_target_pairs={{0,0},{1,1},{2,10},{3,11},{4,4},{5,5},{6,14},{7,15},{8,8},{9,9},{1... | collective-permute-start | bytes 786440 | tf_op jit(solution)/shard_map/ppermute | solution.py:34
  83.4 13.0 %collective-permute-start.18 = (bf16[1024,128]{1,0:T(8,128)(2,1)S(1)}, bf16[1024,128]{1,0:T(8,128)(2,1)S(1)}, u32[]{:S(2)}, u32[]{:S(2)}) collective-permute-start(bf16[1024,128]{1,0:T(8,128)(2,1)S(1)} %get-tuple-element.14), channel_id=1, source_target_pairs={{0,1},{1,0},{2,11},{3,10},{4,5},{5,4},{6,15},{7,14},{8,9},{9,8},{1... | collective-permute-start | bytes 786440 | tf_op jit(solution)/shard_map/ppermute | solution.py:34
  97.2 13.2 %copy-start.3 = (f32[32]{0:T(128)S(1)}, f32[32]{0:T(128)}, u32[]{:S(2)}) copy-start(f32[32]{0:T(128)} %param.6) | copy-start | bytes 388
  97.2 13.4 %copy-start.1 = (f32[256]{0:T(256)S(1)}, f32[256]{0:T(256)}, u32[]{:S(2)}) copy-start(f32[256]{0:T(256)} %param.7) | copy-start | bytes 3076
  97.2 43.4 %collective-permute-start.19 = (bf16[2048,128]{1,0:T(8,128)(2,1)}, bf16[2048,128]{1,0:T(8,128)(2,1)}, u32[]{:S(2)}, u32[]{:S(2)}) collective-permute-start(bf16[2048,128]{1,0:T(8,128)(2,1)} %shard_map.56), channel_id=1, source_target_pairs={{0,0},{1,1},{2,80},{3,81},{4,32},{5,33},{6,112},{7,113},{8,64},{9,... | collective-permute-start | bytes 1572872 | tf_op jit(solution)/shard_map/ppermute | solution.py:34
  103.9 31.0 %collective-permute-start.20 = (bf16[1024,128]{1,0:T(8,128)(2,1)}, bf16[1024,128]{1,0:T(8,128)(2,1)S(1)}, u32[]{:S(2)}, u32[]{:S(2)}) collective-permute-start(bf16[1024,128]{1,0:T(8,128)(2,1)} %get-tuple-element.15), channel_id=1, source_target_pairs={{0,0},{1,1},{2,16},{3,17},{4,32},{5,33},{6,48},{7,49},{8,64},{9,65... | collective-permute-start | bytes 786440 | tf_op jit(solution)/shard_map/ppermute | solution.py:34
  109.4 31.2 %collective-permute-start.21 = (bf16[1024,128]{1,0:T(8,128)(2,1)}, bf16[1024,128]{1,0:T(8,128)(2,1)}, u32[]{:S(2)}, u32[]{:S(2)}) collective-permute-start(bf16[1024,128]{1,0:T(8,128)(2,1)} %get-tuple-element.16), channel_id=1, source_target_pairs={{0,1},{1,0},{2,17},{3,16},{4,33},{5,32},{6,49},{7,48},{8,65},{9,64... | collective-permute-start | bytes 786440 | tf_op jit(solution)/shard_map/ppermute | solution.py:34

commit v2 on v1

--- a/solution.py
+++ b/solution.py
@@ -219,23 +219,30 @@
             spread_rows(share, inverse.at[i * size : (i + 1) * size], j, base.shape[1])
 
 
-def final_kernel(place, base, inverse, early_both, late_same, late_other, out):
+def final_kernel(place, base, inverse, early_both, late_same, late_other, out, done, sems):
     size = late_same.shape[0]
-    for orbital in range(out.shape[0] // size):
+    count = done.shape[0] // size
+    copies = []
+    for orbital in range(count):
         rows = slice(orbital * size, (orbital + 1) * size)
         same = place[0] == orbital // 2
         if orbital % 2 == 0:
             first = pl.ds(pl.multiple_of(jnp.where(same, 0, size), size), size)
-            out[rows, :] = base[rows, :] + early_both[first, :].astype(F32) * inverse[rows, :]
-            continue
-
-        @pl.when(same)
-        def _():
-            out[rows, :] = base[rows, :] + late_same[...].astype(F32) * inverse[rows, :]
-
-        @pl.when(jnp.logical_not(same))
-        def _():
-            out[rows, :] = base[rows, :] + late_other[...].astype(F32) * inverse[rows, :]
+            done[rows, :] = base[rows, :] + early_both[first, :].astype(F32) * inverse[rows, :]
+        else:
+
+            @pl.when(same)
+            def _():
+                done[rows, :] = base[rows, :] + late_same[...].astype(F32) * inverse[rows, :]
+
+            @pl.when(jnp.logical_not(same))
+            def _():
+                done[rows, :] = base[rows, :] + late_other[...].astype(F32) * inverse[rows, :]
+
+        copies.append(pltpu.make_async_copy(done.at[rows, :], out.at[rows, :], sems.at[orbital]))
+        copies[-1].start()
+    for copy in copies:
+        copy.wait()
 
 
 def inner(amplitudes, factors, occ_energy, vir_energy):
@@ -313,7 +320,16 @@
     )(occ_first, occ_second, *operands)
     operands = [place, base, inverse, *mirrored]
     specs = [SMEM] + [VMEM] * (len(operands) - 1)
-    out = call(final_kernel, shape, operands, 2 * shape.size, specs=specs)
+    out = pl.pallas_call(
+        final_kernel,
+        out_shape=shape,
+        in_specs=specs,
+        out_specs=pl.BlockSpec(memory_space=pl.ANY),
+        scratch_shapes=[pltpu.VMEM(shape.shape, F32), pltpu.SemaphoreType.DMA((own_rows,))],
+        compiler_params=pltpu.CompilerParams(vmem_limit_bytes=6 << 20),
+        cost_estimate=pl.CostEstimate(flops=2 * shape.size, bytes_accessed=12 * shape.size, transcendentals=0),
+        name="finish",
+    )(*operands)
     out = out.reshape(own_rows, virtual, cuts, pairs_cols, lanes).transpose(0, 1, 3, 2, 4)
     return out.reshape(own_rows, virtual, pairs_cols, virtual)
 

time: 144 us -> 144 us (level)
    pallas_call x12 -> x11, Pallas kernels: 25.9 us -> 23.2 us  [call(): pl.pallas_call(kernel, out_shape=out_shape, in_specs=specs or [VMEM] * le...]
    pallas_call x0 -> x1, Pallas kernels: none -> 2.54 us  [inner(): pl.pallas_call(final_kernel, out_shape=shape, in_specs=specs, out_specs=p...]
where the time goes in v2:
time: 144 us; the launch traced here: 143 us
  waiting for transfers between devices  72.2 us (50%)
  starting transfers between devices  39.7 us (28%)
  Pallas kernels  29.3 us (20%)
  local copies, waits for them, and re-layouts  1.66 us (1%)
    ppermute x22, waiting for transfers between devices, send(): return lax.ppermute(value, AXES, permutation(move))  72.2 us
    ppermute x22, starting transfers between devices, send(): return lax.ppermute(value, AXES, permutation(move))  39.7 us
    pallas_call x11, Pallas kernels, call(): pl.pallas_call(kernel, out_shape=out_shape, in_specs=specs or [VMEM] * le...  23.2 us
  transfers between devices with their start and end apart: 22, of which 13 were waited for; matrix products, arithmetic and copies ran while one was open for 0% of the time, Pallas kernels for 19%

profile of v2, /device:TPU:13, one launch (start us, length us, event | category | flops | bytes accessed | tf_op | source)
XLA Modules:
  0.0 143.3 jit_solution(11296743236646670910)
XLA Ops:
  0.0 1.0 constant_dynamic-slice_fusion.1
  1.0 1.4 collective-permute-start
  2.4 0.2 collective-permute-start.1
  2.6 2.0 %collective-permute-start.2 = (bf16[1,128,384]{2,1,0:T(8,128)(2,1)S(1)}, bf16[1,128,384]{2,1,0:T(8,128)(2,1)S(1)}, u32[]{:S(2)}, u32[]{:S(2)}) collective-permute-start(bf16[1,128,384]{2,1,0:T(8,128)(2,1)S(1)} %constant_dynamic-slice_fusion.1), channel_id=1, source_target_pairs={{0,32},{1,33},{2,34},{3,35},{4,36},{5,37},{6,38},{7,39},{8,40},{9,... | collective-permute-start | bytes 294920 | tf_op jit(solution)/shard_map/ppermute | solution.py:34
  4.6 0.0 collective-permute-done.refs_0_
  4.6 1.4 collective-permute-done.1.refs_1_
  6.0 2.3 %collective-permute-done.2.refs_2_ = bf16[1,128,384]{2,1,0:T(8,128)(2,1)S(1)} collective-permute-done((bf16[1,128,384]{2,1,0:T(8,128)(2,1)S(1)}, bf16[1,128,384]{2,1,0:T(8,128)(2,1)S(1)}, u32[]{:S(2)}, u32[]{:S(2)}) %collective-permute-start.2) | collective-permute-done | bytes 98336 | tf_op jit(solution)/shard_map/ppermute | solution.py:34
  8.4 1.7 %collective-permute-start.3 = (bf16[3,128,384]{2,1,0:T(8,128)(2,1)S(1)}, bf16[3,128,384]{2,1,0:T(8,128)(2,1)S(1)}, u32[]{:S(2)}, u32[]{:S(2)}) collective-permute-start(bf16[3,128,384]{2,1,0:T(8,128)(2,1)S(1)} %shard_map.47.refs_0_), channel_id=1, source_target_pairs={{0,4},{1,5},{2,6},{3,7},{4,8},{5,9},{6,10},{7,11},{8,12},{9,13},{1... | collective-permute-start | bytes 884744 | tf_op jit(solution)/shard_map/ppermute | solution.py:34
  10.1 3.3 %collective-permute-start.4 = (bf16[3,128,384]{2,1,0:T(8,128)(2,1)S(1)}, bf16[3,128,384]{2,1,0:T(8,128)(2,1)S(1)}, u32[]{:S(2)}, u32[]{:S(2)}) collective-permute-start(bf16[3,128,384]{2,1,0:T(8,128)(2,1)S(1)} %shard_map.47.refs_0_), channel_id=1, source_target_pairs={{0,8},{1,9},{2,10},{3,11},{4,12},{5,13},{6,14},{7,15},{8,0},{9,1},... | collective-permute-start | bytes 884744 | tf_op jit(solution)/shard_map/ppermute | solution.py:34
  13.4 0.7 collective-permute-start.5
  14.1 3.4 %collective-permute-done.3.refs_1_ = bf16[3,128,384]{2,1,0:T(8,128)(2,1)S(1)} collective-permute-done((bf16[3,128,384]{2,1,0:T(8,128)(2,1)S(1)}, bf16[3,128,384]{2,1,0:T(8,128)(2,1)S(1)}, u32[]{:S(2)}, u32[]{:S(2)}) %collective-permute-start.3) | collective-permute-done | bytes 294944 | tf_op jit(solution)/shard_map/ppermute | solution.py:34
  17.5 7.2 %collective-permute-done.4.refs_2_ = bf16[3,128,384]{2,1,0:T(8,128)(2,1)S(1)} collective-permute-done((bf16[3,128,384]{2,1,0:T(8,128)(2,1)S(1)}, bf16[3,128,384]{2,1,0:T(8,128)(2,1)S(1)}, u32[]{:S(2)}, u32[]{:S(2)}) %collective-permute-start.4) | collective-permute-done | bytes 294944 | tf_op jit(solution)/shard_map/ppermute | solution.py:34
  24.7 0.6 collective-permute-done.5.refs_3_
  25.3 0.1 shard_map.48.right_moved
  25.4 2.5 %collective-permute-start.6 = (bf16[12,128,384]{2,1,0:T(8,128)(2,1)S(1)}, bf16[12,128,384]{2,1,0:T(8,128)(2,1)S(1)}, u32[]{:S(2)}, u32[]{:S(2)}) collective-permute-start(bf16[12,128,384]{2,1,0:T(8,128)(2,1)S(1)} %shard_map.48.right_moved), channel_id=1, source_target_pairs={{0,1},{1,0},{2,3},{3,2},{4,5},{5,4},{6,7},{7,6},{8,9},{9,8},{10,11... | collective-permute-start | bytes 3538952 | tf_op jit(solution)/shard_map/ppermute | solution.py:34
  27.9 0.3 collective-permute-start.13
  28.2 0.2 copy.8
  28.4 0.1 fusion
  28.5 0.6 collective-permute-start.7
  29.1 1.0 collective-permute-start.11
  30.1 10.1 %collective-permute-done.13.moved = bf16[2,256,384]{2,1,0:T(8,128)(2,1)S(1)} collective-permute-done((bf16[2,256,384]{2,1,0:T(8,128)(2,1)S(1)}, bf16[2,256,384]{2,1,0:T(8,128)(2,1)S(1)}, u32[]{:S(2)}, u32[]{:S(2)}) %collective-permute-start.13) | collective-permute-done | bytes 393248 | tf_op jit(solution)/shard_map/ppermute | solution.py:34
  40.1 0.9 collective-permute-start.14
  41.0 1.0 collective-permute-start.8
  42.1 0.0 collective-permute-done.7.refs_5_
  42.1 0.4 collective-permute-start.9
  42.5 0.1 pad_add_fusion.place
  42.6 0.0 collective-permute-done.11.refs_6_
  42.6 1.3 collective-permute-start.10
  43.9 0.0 collective-permute-done.14.swapped
  43.9 0.5 collective-permute-start.12
  44.4 1.6 %shard_map.46.refs_0_ = bf16[1024,1024]{1,0:T(8,128)(2,1)S(1)} custom-call(bf16[4,256,384]{2,1,0:T(8,128)(2,1)S(1)} %copy-done, bf16[4,256,384]{2,1,0:T(8,128)(2,1)S(1)} %copy-done), custom_call_target="tpu_custom_call" | custom-call | flops 805306368 | bytes 1048576 | tf_op jit(solution)/shard_map/pallas_call | solution.py:75
  46.0 2.2 %shard_map.52.refs_0_ = bf16[1024,1024]{1,0:T(8,128)(2,1)S(1)} custom-call(s32[2]{0:T(128)S(1)} %pad_add_fusion.place, bf16[2,256,384]{2,1,0:T(8,128)(2,1)S(1)} %collective-permute-done.13.moved, bf16[2,256,384]{2,1,0:T(8,128)(2,1)S(1)} %collective-permute-done.14.swapped, bf16[4,256,384]{2,1,0:T(8,128)(2,1)S(1)} %copy-done), custom_call_target="tpu_custom_call" | custom-call | flops 805306368 | bytes 1048576 | tf_op jit(solution)/shard_map/pallas_call | solution.py:75
  48.2 0.0 collective-permute-done.6.right_swapped
  48.2 4.6 %shard_map.53.refs_1_.refs_2_.refs_3_ = bf16[1024,3072]{1,0:T(8,128)(2,1)S(1)} custom-call(s32[2]{0:T(128)S(1)} %pad_add_fusion.place, bf16[2,256,384]{2,1,0:T(8,128)(2,1)S(1)} %collective-permute-done.13.moved, bf16[2,256,384]{2,1,0:T(8,128)(2,1)S(1)} %collective-permute-done.14.swapped, bf16[12,128,384]{2,1,0:T(8,128)(2,1)S(1)} %shard_map.48.right_moved, ...), custom_call_target="tpu_custom_call" | custom-call | flops 2415919104 | bytes 1048576 | tf_op jit(solution)/shard_map/pallas_call | solution.py:75
  52.8 1.7 %collective-permute-done.8.refs_6_ = bf16[1024,256]{1,0:T(8,128)(2,1)S(1)} collective-permute-done((bf16[1024,256]{1,0:T(8,128)(2,1)S(1)}, bf16[1024,256]{1,0:T(8,128)(2,1)S(1)}, u32[]{:S(2)}, u32[]{:S(2)}) %collective-permute-start.8) | collective-permute-done | bytes 524320 | tf_op jit(solution)/shard_map/ppermute | solution.py:34
  54.5 0.6 collective-permute-done.9.refs_7_
  55.1 2.3 %shard_map.54 = bf16[1024,256]{1,0:T(8,128)(2,1)S(1)} custom-call(bf16[1024,1024]{1,0:T(8,128)(2,1)S(1)} %shard_map.52.refs_0_, bf16[1024,3072]{1,0:T(8,128)(2,1)S(1)} %shard_map.53.refs_1_.refs_2_.refs_3_, bf16[1024,3072]{1,0:T(8,128)(2,1)S(1)} %shard_map.53.refs_1_.refs_2_.refs_3_, bf16[1024,3072]{1,0:T(8,128)(2,1)S(1)} %shard_map.53.refs_1_.refs_2_.refs_3_, ...), custom_call_target="tpu_custom_call" | custom-call | flops 2147483648 | bytes 1048576 | tf_op jit(solution)/shard_map/pallas_call | solution.py:75
  57.5 2.8 %collective-permute-start.15 = (bf16[1024,256]{1,0:T(8,128)(2,1)S(1)}, bf16[1024,256]{1,0:T(8,128)(2,1)S(1)}, u32[]{:S(2)}, u32[]{:S(2)}) collective-permute-start(bf16[1024,256]{1,0:T(8,128)(2,1)S(1)} %shard_map.54), channel_id=1, source_target_pairs={{0,64},{1,65},{2,66},{3,67},{4,68},{5,69},{6,70},{7,71},{8,72},{9,... | collective-permute-start | bytes 1572872 | tf_op jit(solution)/shard_map/ppermute | solution.py:34
  60.3 6.1 %collective-permute-done.10.refs_5_ = bf16[1024,256]{1,0:T(8,128)(2,1)S(1)} collective-permute-done((bf16[1024,256]{1,0:T(8,128)(2,1)S(1)}, bf16[1024,256]{1,0:T(8,128)(2,1)S(1)}, u32[]{:S(2)}, u32[]{:S(2)}) %collective-permute-start.10) | collective-permute-done | bytes 524320 | tf_op jit(solution)/shard_map/ppermute | solution.py:34
  66.4 0.0 collective-permute-done.12.refs_7_
  66.4 2.3 %shard_map.55 = bf16[1024,256]{1,0:T(8,128)(2,1)S(1)} custom-call(bf16[1024,1024]{1,0:T(8,128)(2,1)S(1)} %shard_map.52.refs_0_, bf16[1024,3072]{1,0:T(8,128)(2,1)S(1)} %shard_map.53.refs_1_.refs_2_.refs_3_, bf16[1024,3072]{1,0:T(8,128)(2,1)S(1)} %shard_map.53.refs_1_.refs_2_.refs_3_, bf16[1024,3072]{1,0:T(8,128)(2,1)S(1)} %shard_map.53.refs_1_.refs_2_.refs_3_, ...), custom_call_target="tpu_custom_call" | custom-call | flops 2147483648 | bytes 1048576 | tf_op jit(solution)/shard_map/pallas_call | solution.py:75
  68.7 3.0 %collective-permute-start.16 = (bf16[1024,256]{1,0:T(8,128)(2,1)S(1)}, bf16[1024,256]{1,0:T(8,128)(2,1)S(1)}, u32[]{:S(2)}, u32[]{:S(2)}) collective-permute-start(bf16[1024,256]{1,0:T(8,128)(2,1)S(1)} %shard_map.55), channel_id=1, source_target_pairs={{0,64},{1,65},{2,66},{3,67},{4,68},{5,69},{6,70},{7,71},{8,72},{9,... | collective-permute-start | bytes 1572872 | tf_op jit(solution)/shard_map/ppermute | solution.py:34
  71.7 4.6 %shard_map.49.refs_1_.refs_2_.refs_3_ = bf16[1024,3072]{1,0:T(8,128)(2,1)S(1)} custom-call(s32[2]{0:T(128)S(1)} %pad_add_fusion.place, bf16[4,256,384]{2,1,0:T(8,128)(2,1)S(1)} %copy-done, bf16[12,128,384]{2,1,0:T(8,128)(2,1)S(1)} %shard_map.48.right_moved, bf16[12,128,384]{2,1,0:T(8,128)(2,1)S(1)} %collective-permute-done.6.right_swapped), custom_call_target="tpu_custom_call" | custom-call | flops 2415919104 | bytes 1048576 | tf_op jit(solution)/shard_map/pallas_call | solution.py:75
  76.3 2.3 %shard_map.50.refs_0_.mine = f32[1024,256]{1,0:T(8,128)S(1)} custom-call(bf16[1024,1024]{1,0:T(8,128)(2,1)S(1)} %shard_map.46.refs_0_, bf16[1024,3072]{1,0:T(8,128)(2,1)S(1)} %shard_map.49.refs_1_.refs_2_.refs_3_, bf16[1024,3072]{1,0:T(8,128)(2,1)S(1)} %shard_map.49.refs_1_.refs_2_.refs_3_, bf16[1024,3072]{1,0:T(8,128)(2,1)S(1)} %shard_map.49.refs_1_.refs_2_.refs_3_, ...), custom_call_target="tpu_custom_call" | custom-call | flops 2147483648 | bytes 1048576 | tf_op jit(solution)/shard_map/pallas_call | solution.py:75
  78.6 0.0 collective-permute-done.15.refs_2_.received
  78.7 0.9 round.2
  79.6 3.8 %collective-permute-start.17 = (bf16[1024,128]{1,0:T(8,128)(2,1)S(1)}, bf16[1024,128]{1,0:T(8,128)(2,1)S(1)}, u32[]{:S(2)}, u32[]{:S(2)}) collective-permute-start(bf16[1024,128]{1,0:T(8,128)(2,1)S(1)} %get-tuple-element.13), channel_id=1, source_target_pairs={{0,0},{1,1},{2,10},{3,11},{4,4},{5,5},{6,14},{7,15},{8,8},{9,9},{1... | collective-permute-start | bytes 786440 | tf_op jit(solution)/shard_map/ppermute | solution.py:34
  83.4 3.1 %collective-permute-start.18 = (bf16[1024,128]{1,0:T(8,128)(2,1)S(1)}, bf16[1024,128]{1,0:T(8,128)(2,1)S(1)}, u32[]{:S(2)}, u32[]{:S(2)}) collective-permute-start(bf16[1024,128]{1,0:T(8,128)(2,1)S(1)} %get-tuple-element.14), channel_id=1, source_target_pairs={{0,1},{1,0},{2,11},{3,10},{4,5},{5,4},{6,15},{7,14},{8,9},{9,8},{1... | collective-permute-start | bytes 786440 | tf_op jit(solution)/shard_map/ppermute | solution.py:34
  86.4 2.1 %collective-permute-done.17.refs_0_ = bf16[1024,128]{1,0:T(8,128)(2,1)S(1)} collective-permute-done((bf16[1024,128]{1,0:T(8,128)(2,1)S(1)}, bf16[1024,128]{1,0:T(8,128)(2,1)S(1)}, u32[]{:S(2)}, u32[]{:S(2)}) %collective-permute-start.17) | collective-permute-done | bytes 262176 | tf_op jit(solution)/shard_map/ppermute | solution.py:34
  88.5 7.8 %collective-permute-done.18.refs_1_ = bf16[1024,128]{1,0:T(8,128)(2,1)S(1)} collective-permute-done((bf16[1024,128]{1,0:T(8,128)(2,1)S(1)}, bf16[1024,128]{1,0:T(8,128)(2,1)S(1)}, u32[]{:S(2)}, u32[]{:S(2)}) %collective-permute-start.18) | collective-permute-done | bytes 262176 | tf_op jit(solution)/shard_map/ppermute | solution.py:34
  96.3 0.8 shard_map.56
  97.2 2.8 %collective-permute-start.19 = (bf16[2048,128]{1,0:T(8,128)(2,1)}, bf16[2048,128]{1,0:T(8,128)(2,1)}, u32[]{:S(2)}, u32[]{:S(2)}) collective-permute-start(bf16[2048,128]{1,0:T(8,128)(2,1)} %shard_map.56), channel_id=1, source_target_pairs={{0,0},{1,1},{2,80},{3,81},{4,32},{5,33},{6,112},{7,113},{8,64},{9,... | collective-permute-start | bytes 1572872 | tf_op jit(solution)/shard_map/ppermute | solution.py:34
  99.9 2.3 %shard_map.51.refs_1_.mine = f32[1024,256]{1,0:T(8,128)S(1)} custom-call(bf16[1024,1024]{1,0:T(8,128)(2,1)S(1)} %shard_map.46.refs_0_, bf16[1024,3072]{1,0:T(8,128)(2,1)S(1)} %shard_map.49.refs_1_.refs_2_.refs_3_, bf16[1024,3072]{1,0:T(8,128)(2,1)S(1)} %shard_map.49.refs_1_.refs_2_.refs_3_, bf16[1024,3072]{1,0:T(8,128)(2,1)S(1)} %shard_map.49.refs_1_.refs_2_.refs_3_, ...), custom_call_target="tpu_custom_call" | custom-call | flops 2147483648 | bytes 1048576 | tf_op jit(solution)/shard_map/pallas_call | solution.py:75
  102.3 0.0 collective-permute-done.16.refs_3_.received
  102.3 1.6 %round.3 = (bf16[1024,128]{1,0:T(8,128)(2,1)}, bf16[1024,128]{1,0:T(8,128)(2,1)}) custom-call(s32[2]{0:T(128)S(1)} %pad_add_fusion.place, f32[1024,256]{1,0:T(8,128)S(1)} %shard_map.51.refs_1_.mine, bf16[1024,256]{1,0:T(8,128)(2,1)S(1)} %collective-permute-done.16.refs_3_.received), custom_call_target="tpu_custom_call" | custom-call | flops 262144 | bytes 1572864 | tf_op jit(solution)/shard_map/round/pallas_call | solution.py:196
  103.9 5.5 %collective-permute-start.20 = (bf16[1024,128]{1,0:T(8,128)(2,1)}, bf16[1024,128]{1,0:T(8,128)(2,1)S(1)}, u32[]{:S(2)}, u32[]{:S(2)}) collective-permute-start(bf16[1024,128]{1,0:T(8,128)(2,1)} %get-tuple-element.15), channel_id=1, source_target_pairs={{0,0},{1,1},{2,16},{3,17},{4,32},{5,33},{6,48},{7,49},{8,64},{9,65... | collective-permute-start | bytes 786440 | tf_op jit(solution)/shard_map/ppermute | solution.py:34
  109.4 0.9 collective-permute-start.21
  110.4 0.1 dynamic_slice.12.occ_first
  110.4 0.1 dynamic_slice.13.occ_second
  110.5 0.1 copy.6.vir_col
  110.7 1.1 prepare.1
  111.7 23.1 %collective-permute-done.20.late_same = bf16[1024,128]{1,0:T(8,128)(2,1)S(1)} collective-permute-done((bf16[1024,128]{1,0:T(8,128)(2,1)}, bf16[1024,128]{1,0:T(8,128)(2,1)S(1)}, u32[]{:S(2)}, u32[]{:S(2)}) %collective-permute-start.20) | collective-permute-done | bytes 262176 | tf_op jit(solution)/shard_map/ppermute | solution.py:34
  134.9 5.7 %collective-permute-done.21.late_other = bf16[1024,128]{1,0:T(8,128)(2,1)} collective-permute-done((bf16[1024,128]{1,0:T(8,128)(2,1)}, bf16[1024,128]{1,0:T(8,128)(2,1)}, u32[]{:S(2)}, u32[]{:S(2)}) %collective-permute-start.21) | collective-permute-done | bytes 262176 | tf_op jit(solution)/shard_map/ppermute | solution.py:34
  140.6 2.5 %finish.1 = f32[4096,128]{1,0:T(8,128)} custom-call(s32[2]{0:T(128)S(1)} %pad_add_fusion.place, f32[4096,128]{1,0:T(8,128)S(1)} %get-tuple-element.11.base, f32[4096,128]{1,0:T(8,128)S(1)} %get-tuple-element.12.inverse, bf16[2048,128]{1,0:T(8,128)(2,1)} %collective-permute-done.19.early_both, bf16[1024,128]{1,0:T(8,128)(2,1)S(1)} %collective-permute-done.20.late_same, ...), custom_call_target="tpu_custom_call" | custom-call | flops 1048576 | bytes 6291456 | tf_op jit(solution)/shard_map/finish/pallas_call | solution.py:323
  (11 shorter events, 0.1 us)
Async XLA Ops:
  0.0 27.9 %copy-start = (bf16[4,256,384]{2,1,0:T(8,128)(2,1)S(1)}, bf16[4,256,384]{2,1,0:T(8,128)(2,1)}, u32[]{:S(2)}) copy-start(bf16[4,256,384]{2,1,0:T(8,128)(2,1)} %right.3) | copy-start | bytes 2359300
  0.0 28.2 %copy-start.2 = (bf16[4,256,2,256]{3,2,1,0:T(2,128)(2,1)S(1)}, bf16[4,256,2,256]{3,2,1,0:T(2,128)(2,1)}, u32[]{:S(2)}) copy-start(bf16[4,256,2,256]{3,2,1,0:T(2,128)(2,1)} %param.4) | copy-start | bytes 3145732
  1.0 3.6 %collective-permute-start = (bf16[1,128,384]{2,1,0:T(8,128)(2,1)S(1)}, bf16[1,128,384]{2,1,0:T(8,128)(2,1)S(1)}, u32[]{:S(2)}, u32[]{:S(2)}) collective-permute-start(bf16[1,128,384]{2,1,0:T(8,128)(2,1)S(1)} %constant_dynamic-slice_fusion.1), channel_id=1, source_target_pairs={{0,16},{1,17},{2,18},{3,19},{4,20},{5,21},{6,22},{7,23},{8,24},{9,... | collective-permute-start | bytes 294920 | tf_op jit(solution)/shard_map/ppermute | solution.py:34
  2.4 3.6 %collective-permute-start.1 = (bf16[1,128,384]{2,1,0:T(8,128)(2,1)S(1)}, bf16[1,128,384]{2,1,0:T(8,128)(2,1)S(1)}, u32[]{:S(2)}, u32[]{:S(2)}) collective-permute-start(bf16[1,128,384]{2,1,0:T(8,128)(2,1)S(1)} %constant_dynamic-slice_fusion.1), channel_id=1, source_target_pairs={{0,48},{1,49},{2,50},{3,51},{4,52},{5,53},{6,54},{7,55},{8,56},{9,... | collective-permute-start | bytes 294920 | tf_op jit(solution)/shard_map/ppermute | solution.py:34
  2.6 5.8 %collective-permute-start.2 = (bf16[1,128,384]{2,1,0:T(8,128)(2,1)S(1)}, bf16[1,128,384]{2,1,0:T(8,128)(2,1)S(1)}, u32[]{:S(2)}, u32[]{:S(2)}) collective-permute-start(bf16[1,128,384]{2,1,0:T(8,128)(2,1)S(1)} %constant_dynamic-slice_fusion.1), channel_id=1, source_target_pairs={{0,32},{1,33},{2,34},{3,35},{4,36},{5,37},{6,38},{7,39},{8,40},{9,... | collective-permute-start | bytes 294920 | tf_op jit(solution)/shard_map/ppermute | solution.py:34
  8.4 9.1 %collective-permute-start.3 = (bf16[3,128,384]{2,1,0:T(8,128)(2,1)S(1)}, bf16[3,128,384]{2,1,0:T(8,128)(2,1)S(1)}, u32[]{:S(2)}, u32[]{:S(2)}) collective-permute-start(bf16[3,128,384]{2,1,0:T(8,128)(2,1)S(1)} %shard_map.47.refs_0_), channel_id=1, source_target_pairs={{0,4},{1,5},{2,6},{3,7},{4,8},{5,9},{6,10},{7,11},{8,12},{9,13},{1... | collective-permute-start | bytes 884744 | tf_op jit(solution)/shard_map/ppermute | solution.py:34
  10.1 14.6 %collective-permute-start.4 = (bf16[3,128,384]{2,1,0:T(8,128)(2,1)S(1)}, bf16[3,128,384]{2,1,0:T(8,128)(2,1)S(1)}, u32[]{:S(2)}, u32[]{:S(2)}) collective-permute-start(bf16[3,128,384]{2,1,0:T(8,128)(2,1)S(1)} %shard_map.47.refs_0_), channel_id=1, source_target_pairs={{0,8},{1,9},{2,10},{3,11},{4,12},{5,13},{6,14},{7,15},{8,0},{9,1},... | collective-permute-start | bytes 884744 | tf_op jit(solution)/shard_map/ppermute | solution.py:34
  13.4 11.9 %collective-permute-start.5 = (bf16[3,128,384]{2,1,0:T(8,128)(2,1)S(1)}, bf16[3,128,384]{2,1,0:T(8,128)(2,1)S(1)}, u32[]{:S(2)}, u32[]{:S(2)}) collective-permute-start(bf16[3,128,384]{2,1,0:T(8,128)(2,1)S(1)} %shard_map.47.refs_0_), channel_id=1, source_target_pairs={{0,12},{1,13},{2,14},{3,15},{4,0},{5,1},{6,2},{7,3},{8,4},{9,5},{1... | collective-permute-start | bytes 884744 | tf_op jit(solution)/shard_map/ppermute | solution.py:34
  25.4 22.8 %collective-permute-start.6 = (bf16[12,128,384]{2,1,0:T(8,128)(2,1)S(1)}, bf16[12,128,384]{2,1,0:T(8,128)(2,1)S(1)}, u32[]{:S(2)}, u32[]{:S(2)}) collective-permute-start(bf16[12,128,384]{2,1,0:T(8,128)(2,1)S(1)} %shard_map.48.right_moved), channel_id=1, source_target_pairs={{0,1},{1,0},{2,3},{3,2},{4,5},{5,4},{6,7},{7,6},{8,9},{9,8},{10,11... | collective-permute-start | bytes 3538952 | tf_op jit(solution)/shard_map/ppermute | solution.py:34
  27.9 12.2 %collective-permute-start.13 = (bf16[2,256,384]{2,1,0:T(8,128)(2,1)S(1)}, bf16[2,256,384]{2,1,0:T(8,128)(2,1)S(1)}, u32[]{:S(2)}, u32[]{:S(2)}) collective-permute-start(bf16[2,256,384]{2,1,0:T(8,128)(2,1)S(1)} %constant_dynamic-slice_fusion), channel_id=1, source_target_pairs={{0,64},{1,65},{2,66},{3,67},{4,68},{5,69},{6,70},{7,71},{8,72},{9,... | collective-permute-start | bytes 1179656 | tf_op jit(solution)/shard_map/ppermute | solution.py:34
  28.5 13.5 %collective-permute-start.7 = (bf16[1024,256]{1,0:T(8,128)(2,1)S(1)}, bf16[1024,256]{1,0:T(8,128)(2,1)S(1)}, u32[]{:S(2)}, u32[]{:S(2)}) collective-permute-start(bf16[1024,256]{1,0:T(8,128)(2,1)S(1)} %get-tuple-element.18.refs_4_), channel_id=1, source_target_pairs={{0,16},{1,17},{2,18},{3,19},{4,20},{5,21},{6,22},{7,23},{8,24},{9,... | collective-permute-start | bytes 1572872 | tf_op jit(solution)/shard_map/ppermute | solution.py:34
  29.1 13.5 %collective-permute-start.11 = (bf16[1024,256]{1,0:T(8,128)(2,1)S(1)}, bf16[1024,256]{1,0:T(8,128)(2,1)S(1)}, u32[]{:S(2)}, u32[]{:S(2)}) collective-permute-start(bf16[1024,256]{1,0:T(8,128)(2,1)S(1)} %get-tuple-element.17.refs_4_), channel_id=1, source_target_pairs={{0,48},{1,49},{2,50},{3,51},{4,52},{5,53},{6,54},{7,55},{8,56},{9,... | collective-permute-start | bytes 1572872 | tf_op jit(solution)/shard_map/ppermute | solution.py:34
  40.1 3.8 %collective-permute-start.14 = (bf16[2,256,384]{2,1,0:T(8,128)(2,1)S(1)}, bf16[2,256,384]{2,1,0:T(8,128)(2,1)S(1)}, u32[]{:S(2)}, u32[]{:S(2)}) collective-permute-start(bf16[2,256,384]{2,1,0:T(8,128)(2,1)S(1)} %collective-permute-done.13.moved), channel_id=1, source_target_pairs={{0,1},{1,0},{2,3},{3,2},{4,5},{5,4},{6,7},{7,6},{8,9},{9,8},{10,11... | collective-permute-start | bytes 1179656 | tf_op jit(solution)/shard_map/ppermute | solution.py:34
  41.0 13.5 %collective-permute-start.8 = (bf16[1024,256]{1,0:T(8,128)(2,1)S(1)}, bf16[1024,256]{1,0:T(8,128)(2,1)S(1)}, u32[]{:S(2)}, u32[]{:S(2)}) collective-permute-start(bf16[1024,256]{1,0:T(8,128)(2,1)S(1)} %get-tuple-element.18.refs_4_), channel_id=1, source_target_pairs={{0,48},{1,49},{2,50},{3,51},{4,52},{5,53},{6,54},{7,55},{8,56},{9,... | collective-permute-start | bytes 1572872 | tf_op jit(solution)/shard_map/ppermute | solution.py:34
  42.1 13.1 %collective-permute-start.9 = (bf16[1024,256]{1,0:T(8,128)(2,1)S(1)}, bf16[1024,256]{1,0:T(8,128)(2,1)S(1)}, u32[]{:S(2)}, u32[]{:S(2)}) collective-permute-start(bf16[1024,256]{1,0:T(8,128)(2,1)S(1)} %collective-permute-done.7.refs_5_), channel_id=1, source_target_pairs={{0,16},{1,17},{2,18},{3,19},{4,20},{5,21},{6,22},{7,23},{8,24},{9,... | collective-permute-start | bytes 1572872 | tf_op jit(solution)/shard_map/ppermute | solution.py:34
  42.6 23.8 %collective-permute-start.10 = (bf16[1024,256]{1,0:T(8,128)(2,1)S(1)}, bf16[1024,256]{1,0:T(8,128)(2,1)S(1)}, u32[]{:S(2)}, u32[]{:S(2)}) collective-permute-start(bf16[1024,256]{1,0:T(8,128)(2,1)S(1)} %get-tuple-element.17.refs_4_), channel_id=1, source_target_pairs={{0,16},{1,17},{2,18},{3,19},{4,20},{5,21},{6,22},{7,23},{8,24},{9,... | collective-permute-start | bytes 1572872 | tf_op jit(solution)/shard_map/ppermute | solution.py:34
  43.9 22.5 %collective-permute-start.12 = (bf16[1024,256]{1,0:T(8,128)(2,1)S(1)}, bf16[1024,256]{1,0:T(8,128)(2,1)S(1)}, u32[]{:S(2)}, u32[]{:S(2)}) collective-permute-start(bf16[1024,256]{1,0:T(8,128)(2,1)S(1)} %collective-permute-done.11.refs_6_), channel_id=1, source_target_pairs={{0,48},{1,49},{2,50},{3,51},{4,52},{5,53},{6,54},{7,55},{8,56},{9,... | collective-permute-start | bytes 1572872 | tf_op jit(solution)/shard_map/ppermute | solution.py:34
  57.5 21.2 %collective-permute-start.15 = (bf16[1024,256]{1,0:T(8,128)(2,1)S(1)}, bf16[1024,256]{1,0:T(8,128)(2,1)S(1)}, u32[]{:S(2)}, u32[]{:S(2)}) collective-permute-start(bf16[1024,256]{1,0:T(8,128)(2,1)S(1)} %shard_map.54), channel_id=1, source_target_pairs={{0,64},{1,65},{2,66},{3,67},{4,68},{5,69},{6,70},{7,71},{8,72},{9,... | collective-permute-start | bytes 1572872 | tf_op jit(solution)/shard_map/ppermute | solution.py:34
  68.7 33.6 %collective-permute-start.16 = (bf16[1024,256]{1,0:T(8,128)(2,1)S(1)}, bf16[1024,256]{1,0:T(8,128)(2,1)S(1)}, u32[]{:S(2)}, u32[]{:S(2)}) collective-permute-start(bf16[1024,256]{1,0:T(8,128)(2,1)S(1)} %shard_map.55), channel_id=1, source_target_pairs={{0,64},{1,65},{2,66},{3,67},{4,68},{5,69},{6,70},{7,71},{8,72},{9,... | collective-permute-start | bytes 1572872 | tf_op jit(solution)/shard_map/ppermute | solution.py:34
  79.6 8.9 %collective-permute-start.17 = (bf16[1024,128]{1,0:T(8,128)(2,1)S(1)}, bf16[1024,128]{1,0:T(8,128)(2,1)S(1)}, u32[]{:S(2)}, u32[]{:S(2)}) collective-permute-start(bf16[1024,128]{1,0:T(8,128)(2,1)S(1)} %get-tuple-element.13), channel_id=1, source_target_pairs={{0,0},{1,1},{2,10},{3,11},{4,4},{5,5},{6,14},{7,15},{8,8},{9,9},{1... | collective-permute-start | bytes 786440 | tf_op jit(solution)/shard_map/ppermute | solution.py:34
  83.4 13.0 %collective-permute-start.18 = (bf16[1024,128]{1,0:T(8,128)(2,1)S(1)}, bf16[1024,128]{1,0:T(8,128)(2,1)S(1)}, u32[]{:S(2)}, u32[]{:S(2)}) collective-permute-start(bf16[1024,128]{1,0:T(8,128)(2,1)S(1)} %get-tuple-element.14), channel_id=1, source_target_pairs={{0,1},{1,0},{2,11},{3,10},{4,5},{5,4},{6,15},{7,14},{8,9},{9,8},{1... | collective-permute-start | bytes 786440 | tf_op jit(solution)/shard_map/ppermute | solution.py:34
  97.2 13.2 %copy-start.3 = (f32[32]{0:T(128)S(1)}, f32[32]{0:T(128)}, u32[]{:S(2)}) copy-start(f32[32]{0:T(128)} %param.6) | copy-start | bytes 388
  97.2 13.4 %copy-start.1 = (f32[256]{0:T(256)S(1)}, f32[256]{0:T(256)}, u32[]{:S(2)}) copy-start(f32[256]{0:T(256)} %param.7) | copy-start | bytes 3076
  97.2 43.4 %collective-permute-start.19 = (bf16[2048,128]{1,0:T(8,128)(2,1)}, bf16[2048,128]{1,0:T(8,128)(2,1)}, u32[]{:S(2)}, u32[]{:S(2)}) collective-permute-start(bf16[2048,128]{1,0:T(8,128)(2,1)} %shard_map.56), channel_id=1, source_target_pairs={{0,0},{1,1},{2,80},{3,81},{4,32},{5,33},{6,112},{7,113},{8,64},{9,... | collective-permute-start | bytes 1572872 | tf_op jit(solution)/shard_map/ppermute | solution.py:34
  103.9 31.0 %collective-permute-start.20 = (bf16[1024,128]{1,0:T(8,128)(2,1)}, bf16[1024,128]{1,0:T(8,128)(2,1)S(1)}, u32[]{:S(2)}, u32[]{:S(2)}) collective-permute-start(bf16[1024,128]{1,0:T(8,128)(2,1)} %get-tuple-element.15), channel_id=1, source_target_pairs={{0,0},{1,1},{2,16},{3,17},{4,32},{5,33},{6,48},{7,49},{8,64},{9,65... | collective-permute-start | bytes 786440 | tf_op jit(solution)/shard_map/ppermute | solution.py:34
  109.4 31.2 %collective-permute-start.21 = (bf16[1024,128]{1,0:T(8,128)(2,1)}, bf16[1024,128]{1,0:T(8,128)(2,1)}, u32[]{:S(2)}, u32[]{:S(2)}) collective-permute-start(bf16[1024,128]{1,0:T(8,128)(2,1)} %get-tuple-element.16), channel_id=1, source_target_pairs={{0,1},{1,0},{2,17},{3,16},{4,33},{5,32},{6,49},{7,48},{8,65},{9,64... | collective-permute-start | bytes 786440 | tf_op jit(solution)/shard_map/ppermute | solution.py:34
